TPU v7x, 32 devices: a whole 2x2x4 slice. The times are simulated.
32 devices in a mesh: groups: 2 (over y), blk: 4 (over z), det: 2 (over x), sub: 2 (over core).
Axes of the slice: x: 2, y: 2, z: 4, core: 2. Of those that a mesh axis runs over, the one named last changes fastest.
Arguments:
- data: bfloat16 [128, 16, 256], P(('groups', 'blk', 'det')), parts along dimension 0, may hold values from -6 to 6
- templates: bfloat16 [32, 16, 256], P(('groups', 'blk')), parts along dimension 0
- bin_cuts: int32 [32, 15], P(('groups', 'blk')), parts along dimension 0, may hold values from 1 to 2047, as said below
- trig_template: int32 [16, 2, 128], P(('groups', 'blk', 'det'), 'sub'), parts along dimension 0, may hold values from 0 to 15
- trig_pair: int32 [16, 2, 128], P(('groups', 'blk', 'det'), 'sub'), parts along dimension 0, may hold values from 0 to 63, as said below
- trig_tile: int32 [16, 2, 128], P(('groups', 'blk', 'det'), 'sub'), parts along dimension 0, may hold values from 0 to 7
Outputs:
- peak_snr: float32 [128, 2048], P(('groups', 'blk', 'det'), 'sub'), parts along dimension 0
- chi_snr: float32 [16, 2, 128, 128], P(('groups', 'blk', 'det'), 'sub'), parts along dimension 0
There are 2 independent parts, one for each index of `groups`. A program takes and returns all parts, laid end to end along the dimension named above; each array names one. Nothing has to cross between parts.
Inputs may be any that keep to these rules, and one draw needn't show every extreme that they name: `trig_pair`: in each list [b, h], at most 32 entries lie in any one group of 8 consecutive data block ids that starts at a multiple of 8; one such group holds exactly 32 entries of every list. `bin_cuts`: each row is strictly increasing.
All inputs are finite; a program needn't handle non-finite values.
Results may differ from a plain program's by a relative error of at most 0.0035.
Values may be sent and summed in bfloat16 or wider, within the bound.
A program may use at most 64 MiB of HBM per device.

v0:
```python
import math

import jax
import jax.numpy as jnp
from jax import lax
from jax.sharding import PartitionSpec as P

TILE_STEPS = 8


def largest_divisor(count, limit):
    for width in range(min(count, limit), 0, -1):
        return width
    return 1


def phase_table(rows, cols, period):
    index = (
        jnp.arange(rows, dtype=jnp.int32)[:, None]
        * jnp.arange(cols, dtype=jnp.int32)[None, :]
        % period
    )
    angle = index.astype(jnp.float32) * (2.0 * math.pi / period)
    return (jnp.cos(angle), jnp.sin(angle))


def second_matrix(steps, n_minor):
    index = jnp.arange(n_minor, dtype=jnp.int32)[:, None] * steps[None, :] % n_minor
    angle = index.astype(jnp.float32) * (2.0 * math.pi / n_minor)
    cosine = jnp.cos(angle)
    sine = jnp.sin(angle)
    upper = jnp.concatenate([cosine, sine], axis=1)
    lower = jnp.concatenate([-sine, cosine], axis=1)
    return jnp.concatenate([upper, lower], axis=0).astype(jnp.bfloat16)


def make_tables(n_major, n_minor):
    cos_major, sin_major = phase_table(n_major, n_major, n_major)
    twid_cos, twid_sin = phase_table(n_major, n_minor, n_major * n_minor)
    return (cos_major.astype(jnp.bfloat16), sin_major.astype(jnp.bfloat16), twid_cos, twid_sin)


def conj_product(rows, tmpl):
    n_minor = rows.shape[-1] // 2
    data_re = rows[..., :n_minor].astype(jnp.float32)
    data_im = rows[..., n_minor:].astype(jnp.float32)
    tmpl_re = tmpl[..., :n_minor].astype(jnp.float32)
    tmpl_im = tmpl[..., n_minor:].astype(jnp.float32)
    real_part = data_re * tmpl_re + data_im * tmpl_im
    imag_part = data_im * tmpl_re - data_re * tmpl_im
    return jnp.concatenate([real_part, imag_part], axis=-1).astype(jnp.bfloat16)


def first_section(spectra, tables):
    cos_major, sin_major, twid_cos, twid_sin = tables
    n_minor = spectra.shape[-1] // 2
    cos_part = jnp.einsum("...ic,ia->...ac", spectra, cos_major, preferred_element_type=jnp.float32)
    sin_part = jnp.einsum("...ic,ia->...ac", spectra, sin_major, preferred_element_type=jnp.float32)
    real_part = cos_part[..., :n_minor] - sin_part[..., n_minor:]
    imag_part = sin_part[..., :n_minor] + cos_part[..., n_minor:]
    turned_re = real_part * twid_cos - imag_part * twid_sin
    turned_im = real_part * twid_sin + imag_part * twid_cos
    return jnp.concatenate([turned_re, turned_im], axis=-1).astype(jnp.bfloat16)


def chi_block(rows, tmpl, cuts, starts, tables, n_bins, n_steps):
    n_major = rows.shape[1]
    n_minor = rows.shape[2] // 2
    spectra = conj_product(rows, tmpl)
    freq = (
        n_minor * jnp.arange(n_major, dtype=jnp.int32)[:, None]
        + jnp.arange(n_minor, dtype=jnp.int32)[None, :]
    )
    which = jnp.sum((cuts[:, :, None, None] <= freq[None, None]).astype(jnp.int32), axis=1)
    member = which[:, None] == jnp.arange(n_bins, dtype=jnp.int32)[None, :, None, None]
    member = jnp.concatenate([member, member], axis=-1)
    masked = jnp.where(member, spectra[:, None], jnp.zeros((), jnp.bfloat16))
    sectioned = first_section(masked, tables)
    steps = starts[:, None] + jnp.arange(n_steps, dtype=jnp.int32)[None, :]
    mats = jax.vmap(lambda values: second_matrix(values, n_minor))(steps)
    binned = jnp.einsum("rbac,rcs->rbas", sectioned, mats, preferred_element_type=jnp.float32)
    bin_re = binned[..., :n_steps]
    bin_im = binned[..., n_steps:]
    total_re = jnp.sum(bin_re, axis=1)
    total_im = jnp.sum(bin_im, axis=1)
    norms = jnp.sum(jnp.square(tmpl.astype(jnp.float32)), axis=(1, 2))
    diff_re = bin_re - total_re[:, None] / n_bins
    diff_im = bin_im - total_im[:, None] / n_bins
    chisq = n_bins * jnp.sum(diff_re * diff_re + diff_im * diff_im, axis=1) / norms[:, None, None]
    reduced = chisq / (2.0 * n_bins - 2.0)
    rho = jnp.sqrt(total_re * total_re + total_im * total_im) / jnp.sqrt(norms)[:, None, None]
    weighted = jnp.where(reduced > 1.0, rho * ((1.0 + reduced**3) * 0.5) ** (-1.0 / 6.0), rho)
    return jnp.transpose(weighted, (0, 2, 1)).reshape(rows.shape[0], -1)


def chi_rows(rows, tmpl, cuts, starts, tables):
    count = rows.shape[0]
    width = largest_divisor(count, 8)
    groups = count // width
    n_bins = cuts.shape[1] + 1

    def chi_one_group(packed):
        return chi_block(packed[0], packed[1], packed[2], packed[3], tables, n_bins, TILE_STEPS)

    result = lax.map(
        chi_one_group,
        (
            rows.reshape((groups, width) + rows.shape[1:]),
            tmpl.reshape((groups, width) + tmpl.shape[1:]),
            cuts.reshape(groups, width, -1),
            starts.reshape(groups, width),
        ),
    )
    return result.reshape(count, -1)


def peak_update(peak, tmpl, data, tables, second):
    count = tmpl.shape[0]
    width = largest_divisor(count, 8)
    groups = count // width
    n_half = second.shape[1] // 2

    def peak_one_group(block):
        spectra = conj_product(data[None], block[:, None])
        sectioned = first_section(spectra, tables)
        result = jnp.einsum(
            "...ac,cs->...as", sectioned, second, preferred_element_type=jnp.float32
        )
        power = result[..., :n_half] ** 2 + result[..., n_half:] ** 2
        norms = jnp.sum(jnp.square(block.astype(jnp.float32)), axis=(1, 2))
        return jnp.max(power / norms[:, None, None, None], axis=0)

    found = lax.map(peak_one_group, tmpl.reshape((groups, width) + tmpl.shape[1:]))
    return jnp.maximum(peak, jnp.max(found, axis=0))


def select_fold(wanted, data, tables, second, carry, pieces):
    peak, chosen, chosen_cuts = carry
    piece_tmpl, piece_cuts = pieces
    count = piece_tmpl.shape[0]
    peak = peak_update(peak, piece_tmpl, data, tables, second)
    inside = (wanted >= 0) & (wanted < count)
    position = jnp.clip(wanted, 0, count - 1)
    chosen = jnp.where(inside[:, None, None], piece_tmpl[position], chosen)
    chosen_cuts = jnp.where(inside[:, None], piece_cuts[position], chosen_cuts)
    return (peak, chosen, chosen_cuts)


def body(data, templates, bin_cuts, trig_template, trig_pair, trig_tile):
    n_major = data.shape[1]
    n_minor = data.shape[2] // 2
    n_sub = lax.axis_size("sub")
    half_index = lax.axis_index("sub")
    n_half = n_minor // n_sub
    n_groups = lax.axis_size("blk") * lax.axis_size("det")
    pairs_local = data.shape[0]
    tables = make_tables(n_major, n_minor)
    second = second_matrix(half_index * n_half + jnp.arange(n_half, dtype=jnp.int32), n_minor)
    tmpl_ids = trig_template.reshape(-1)
    pair_ids = trig_pair.reshape(-1)
    tile_ids = trig_tile.reshape(-1)
    trig_count = tmpl_ids.shape[0]
    starts = half_index * n_half + tile_ids * TILE_STEPS
    empty_peak = jnp.zeros((pairs_local, n_major, n_half), jnp.float32)
    home = pair_ids // pairs_local
    local_pair = pair_ids % pairs_local
    capacity = 2 * trig_count // n_groups
    onehot = (home[:, None] == jnp.arange(n_groups, dtype=jnp.int32)[None, :]).astype(jnp.int32)
    rank = jnp.sum(jnp.cumsum(onehot, axis=0) * onehot, axis=1) - 1
    slot = home * capacity + rank
    start_carry = (
        empty_peak,
        jnp.zeros((trig_count,) + templates.shape[1:], jnp.bfloat16),
        jnp.zeros((trig_count, bin_cuts.shape[1]), jnp.int32),
    )
    peak, chosen, chosen_cuts = select_fold(
        tmpl_ids,
        data,
        tables,
        second,
        start_carry,
        (
            lax.all_gather(templates, "blk", axis=0, tiled=True),
            lax.all_gather(bin_cuts, "blk", axis=0, tiled=True),
        ),
    )
    send_meta = (
        jnp.zeros((n_groups * capacity, 3), jnp.int32)
        .at[slot]
        .set(jnp.stack([local_pair, local_pair, local_pair], axis=1))
    )
    wanted_rows = data[
        lax.all_to_all(
            send_meta.reshape(n_groups, capacity, 3),
            ("blk", "det"),
            split_axis=0,
            concat_axis=0,
            tiled=True,
        )[..., 0]
    ]
    fetched = lax.all_to_all(wanted_rows, ("blk", "det"), split_axis=0, concat_axis=0, tiled=True)
    trig_rows = fetched.reshape((n_groups * capacity,) + data.shape[1:])[slot]
    chi = chi_rows(trig_rows, chosen, chosen_cuts, starts, tables)
    peak_snr = jnp.transpose(jnp.sqrt(peak), (0, 2, 1)).reshape(pairs_local, n_half * n_major)
    chi_snr = chi.reshape(trig_template.shape + (chi.shape[1],))
    return (peak_snr, chi_snr)


def solution(mesh):
    return jax.shard_map(
        body,
        mesh=mesh,
        in_specs=(
            P(("groups", "blk", "det"), None, None),
            P(("groups", "blk"), None, None),
            P(("groups", "blk"), None),
            P(("groups", "blk", "det"), "sub", None),
            P(("groups", "blk", "det"), "sub", None),
            P(("groups", "blk", "det"), "sub", None),
        ),
        out_specs=(
            P(("groups", "blk", "det"), "sub"),
            P(("groups", "blk", "det"), "sub", None, None),
        ),
        check_vma=False,
    )
```

profile of v0, /device:TPU:0, one launch (start us, length us, event | category | flops | bytes accessed | tf_op | source)
XLA Modules:
  0.0 167.2 jit_solution(16538561163839680892)
XLA Ops:
  4.2 7.3 %all-to-all-start = ((s32[8,32,3]{1,2,0:T(4,128)}), s32[8,32,3]{1,2,0:T(4,128)S(1)}, u32[]{:S(2)}, u32[]{:S(2)}) async-start(s32[8,32,3]{1,2,0:T(4,128)} %copy.12), calls=%async_computation | async-start | bytes 32768 | tf_op jit(solution)/shard_map/all_to_all | solution.py:193
  11.8 14.2 %all_gather.6 = bf16[16,16,256]{2,1,0:T(8,128)(2,1)S(1)} all-gather(bf16[4,16,256]{2,1,0:T(8,128)(2,1)} %param.11), channel_id=1, replica_groups=mesh['groups'=2,'blk'=4,'det'=2,'sub'=2] {'blk'}, dimensions={0}, use_global_device_ids=true | all-gather | bytes 163840 | tf_op jit(solution)/shard_map/all_gather | solution.py:183
  26.1 2.1 %gather_fusion.1 = bf16[256,16,256]{2,1,0:T(8,128)(2,1)} fusion(bf16[8,16,256]{2,1,0:T(8,128)(2,1)S(1)} %copy-done, s32[1024]{0:T(1024)S(1)} %pad_clamp_fusion.1), kind=kCustom, calls=%fused_computation.1 | custom fusion | bytes 4195328 | tf_op jit(solution)/shard_map/gather | solution.py:192
  28.2 5.7 %all-to-all-start.1 = ((bf16[8,32,16,256]{3,2,1,0:T(8,128)(2,1)}), bf16[8,32,16,256]{3,2,1,0:T(8,128)(2,1)S(1)}, u32[]{:S(2)}, u32[]{:S(2)}) async-start(bf16[8,32,16,256]{3,2,1,0:T(8,128)(2,1)} %bitcast.12), calls=%async_computation.1 | async-start | bytes 4194304 | tf_op jit(solution)/shard_map/all_to_all | solution.py:201
  33.9 3.6 %while.26 = (s32[]{:T(128)}, f32[2,8,16,64]{3,2,1,0:T(8,128)S(1)}, bf16[8,16,256]{2,1,0:T(8,128)(2,1)S(1)}, bf16[2,8,16,256]{3,2,1,0:T(8,128)(2,1)S(1)}, bf16[256,128]{1,0:T(8,128)(2,1)S(1)}, /*index=5*/s32[]{:T(128)}) while((s32[]{:T(128)}, f32[2,8,16,64]{3,2,1,0:T(8,128)S(1)}, bf16[8,16,256]{2,1,0:T(8,128)(2,1)S(1)}, ...), condition=%wide.region_3.4_spmd.clone.clone, body=%wide.region_0.3_spmd.clone.clone.sunk | while | flops 89910776 | bytes 8978585 | solution.py:133
  39.2 44.9 %all-gather = s32[4,4,15]{2,1,0:T(4,128)S(1)} all-gather(s32[1,4,15]{2,1,0:T(4,128)S(1)} %bitcast.175), channel_id=1, replica_groups=mesh['groups'=2,'blk'=4,'det'=2,'sub'=2] {'blk'}, dimensions={0}, use_global_device_ids=true | all-gather | bytes 1200 | tf_op jit(solution)/shard_map/all_gather | solution.py:184
  85.1 1.2 broadcast_select_fusion
  86.9 79.7 %while.27 = (s32[]{:T(128)}, f32[16,8,128]{2,1,0:T(8,128)S(1)}, s32[16,8,15]{2,1,0:T(8,128)S(1)}, bf16[16,8,16,256]{3,2,1,0:T(8,128)(2,1)S(1)}, bf16[16,8,16,256...) while((s32[]{:T(128)}, f32[16,8,128]{2,1,0:T(8,128)S(1)}, ...), condition=%wide.region_14.15_spmd.clone.clone, body=%wide.region_8.14_spmd.clone.clone.sunk | while | flops 59148872 | bytes 12736905 | solution.py:105
  90.1 1.3 fusion.170
  95.1 1.3 fusion.170
  100.1 1.3 fusion.170
  105.1 1.3 fusion.170
  110.0 1.3 fusion.170
  115.0 1.3 fusion.170
  120.0 1.3 fusion.170
  125.0 1.3 fusion.170
  129.9 1.3 fusion.170
  134.9 1.3 fusion.170
  139.9 1.3 fusion.170
  144.9 1.3 fusion.170
  149.8 1.3 fusion.170
  154.8 1.3 fusion.170
  159.8 1.3 fusion.170
  164.8 1.3 fusion.170
  (450 shorter events, 68.0 us)
Async XLA Ops:
  0.6 25.5 %copy-start = (bf16[8,16,256]{2,1,0:T(8,128)(2,1)S(1)}, bf16[8,16,256]{2,1,0:T(8,128)(2,1)}, u32[]{:S(2)}) copy-start(bf16[8,16,256]{2,1,0:T(8,128)(2,1)} %param.10) | copy-start | bytes 196612
  4.2 21.8 %all-to-all-start = ((s32[8,32,3]{1,2,0:T(4,128)}), s32[8,32,3]{1,2,0:T(4,128)S(1)}, u32[]{:S(2)}, u32[]{:S(2)}) async-start(s32[8,32,3]{1,2,0:T(4,128)} %copy.12), calls=%async_computation | async-start | bytes 32768 | tf_op jit(solution)/shard_map/all_to_all | solution.py:193
  28.2 58.1 %all-to-all-start.1 = ((bf16[8,32,16,256]{3,2,1,0:T(8,128)(2,1)}), bf16[8,32,16,256]{3,2,1,0:T(8,128)(2,1)S(1)}, u32[]{:S(2)}, u32[]{:S(2)}) async-start(bf16[8,32,16,256]{3,2,1,0:T(8,128)(2,1)} %bitcast.12), calls=%async_computation.1 | async-start | bytes 4194304 | tf_op jit(solution)/shard_map/all_to_all | solution.py:201
  33.9 4.6 %copy-start.3 = (s32[1,1,128]{2,1,0:T(1,128)S(1)}, s32[1,1,128]{2,1,0:T(1,128)}, u32[]{:S(2)}) copy-start(s32[1,1,128]{2,1,0:T(1,128)} %param.13) | copy-start | bytes 1540
  37.5 1.7 copy-start.1
  37.5 47.3 %copy-start.4 = (s32[1,1,128]{2,1,0:T(1,128)S(1)}, s32[1,1,128]{2,1,0:T(1,128)}, u32[]{:S(2)}) copy-start(s32[1,1,128]{2,1,0:T(1,128)} %param.15) | copy-start | bytes 1540
  166.6 0.6 copy-start.2
where the time goes:
time: 168 us; the launch traced here: 167 us
  blocking collectives  59.1 us (35%)
  other arithmetic  45.3 us (27%)
  matrix products  37.9 us (23%)
  starting transfers between devices  12.9 us (8%)
  local copies, waits for them, and re-layouts  9.29 us (6%)
  loops' own time  1.92 us (1%)
    all_gather x1, blocking collectives, body(): lax.all_gather(bin_cuts, 'blk', axis=0, tiled=True)  44.9 us
    dot_general x16, matrix products, chi_block(): jnp.einsum('rbac,rcs->rbas', sectioned, mats, preferred_element_type=jnp....  21.2 us
    reduce_sum x16, other arithmetic, chi_block(): norms = jnp.sum(jnp.square(tmpl.astype(jnp.float32)), axis=(1, 2))  15.9 us
    all_gather x1, blocking collectives, body(): lax.all_gather(templates, 'blk', axis=0, tiled=True)  14.2 us
    another operation x53, other arithmetic  10.9 us
    dot_general x18, matrix products, first_section(): jnp.einsum('...ic,ia->...ac', spectra, cos_major, preferred_element_type=...  8.05 us
    dot_general x18, matrix products, first_section(): jnp.einsum('...ic,ia->...ac', spectra, sin_major, preferred_element_type=...  8.03 us
    all_to_all x1, starting transfers between devices, body(): lax.all_to_all(send_meta.reshape(n_groups, capacity, 3), ('blk', 'det'),...  7.25 us
  transfers between devices with their start and end apart: 2, of which 0 were waited for; matrix products, arithmetic and copies ran while one was open for 5% of the time, Pallas kernels for 0%

commit v1 on v0

v1 whole, which is shorter than its diff:
```python
import functools
import math

import jax
import jax.numpy as jnp
import numpy as np
from jax import lax
from jax.experimental import pallas as pl
from jax.experimental.pallas import tpu as pltpu
from jax.sharding import PartitionSpec as P

MESH = pl.DeviceIdType.MESH
NMAJ = 16
NMIN = 128
NCUT = 16
STEPS = 8
GROUP = 8


def unit_circle(index, period):
    angle = (index % period) * (2.0 * math.pi / period)
    return np.cos(angle), np.sin(angle)


def host_tables(n_sub):
    bf16 = jnp.bfloat16
    major = np.arange(NMAJ)
    minor = np.arange(NMIN)
    cos16, sin16 = unit_circle(major[:, None] * major[None, :], NMAJ)
    eye = np.eye(GROUP)
    first = np.concatenate([np.kron(eye, cos16), np.kron(eye, sin16)], axis=1).astype(bf16)
    twc, tws = unit_circle(major[:, None] * minor[None, :], NMAJ * NMIN)
    twiddle = np.concatenate([twc, tws], axis=1).astype(np.float32)
    n_half = NMIN // n_sub
    second = []
    for half in range(n_sub):
        steps = half * n_half + np.arange(n_half)
        cosine, sine = unit_circle(steps[:, None] * minor[None, :], NMIN)
        real_rows = np.concatenate([cosine, -sine], axis=1)
        imag_rows = np.concatenate([sine, cosine], axis=1)
        second.append(np.concatenate([real_rows, imag_rows], axis=0))
    second = np.stack(second).astype(bf16)
    times = np.arange(NMAJ * STEPS)
    cosine, sine = unit_circle(minor[:, None] * times[None, :], NMAJ * NMIN)
    tile_dft = np.concatenate(
        [np.concatenate([cosine, sine], axis=1), np.concatenate([-sine, cosine], axis=1)], axis=0
    ).astype(bf16)
    rowc, rows = unit_circle(major[:, None] * (times % NMAJ)[None, :], NMAJ)
    row_phase = np.tile(np.concatenate([rowc, rows], axis=1), (GROUP, 1)).astype(bf16)
    starts = np.arange(NMIN // STEPS) * STEPS
    phc, phs = unit_circle(starts[:, None] * minor[None, :], NMIN)
    tile_phase = np.concatenate([phc, phs], axis=1).astype(np.float32)[:, None, :]
    return first, twiddle, second, tile_dft, row_phase, tile_phase


def gather_kernel(n_blk, n_det, n_sub, data, tmpl, cuts, data_out, tmpl_out, cuts_out,
                  local_sem, z_send, z_recv, x_send, x_recv, s_send, s_recv,
                  tz_send, tz_recv, ts_send, ts_recv, cz_send, cz_recv):
    b = lax.axis_index("blk")
    d = lax.axis_index("det")
    c = lax.axis_index("sub")
    pairs = data.shape[0]
    kb = tmpl.shape[0]
    hp, hk = pairs // n_sub, kb // n_sub
    other = n_sub - 1 - c

    barrier = pltpu.get_barrier_semaphore()
    for dz in range(1, n_blk):
        pl.semaphore_signal(barrier, inc=1, device_id={"blk": lax.rem(b + dz, n_blk)}, device_id_type=MESH)
    for dx in range(1, n_det):
        pl.semaphore_signal(barrier, inc=1, device_id={"det": lax.rem(d + dx, n_det)}, device_id_type=MESH)
    pl.semaphore_signal(barrier, inc=1, device_id={"sub": other}, device_id_type=MESH)

    own = b * n_det + d
    locals_ = [
        pltpu.make_async_copy(data, data_out.at[own], local_sem.at[0]),
        pltpu.make_async_copy(tmpl, tmpl_out.at[b], local_sem.at[1]),
        pltpu.make_async_copy(cuts, cuts_out.at[b], local_sem.at[2]),
    ]
    for copy in locals_:
        copy.start()
    pl.semaphore_wait(barrier, n_blk + n_det - 1)

    def remote(src, dst, send, recv, where):
        copy = pltpu.make_async_remote_copy(src_ref=src, dst_ref=dst, send_sem=send, recv_sem=recv,
                                            device_id=where, device_id_type=MESH)
        copy.start()
        return copy

    half_p = pl.ds(c * hp, hp)
    half_k = pl.ds(c * hk, hk)
    z_copies, t_copies, c_copies = {}, {}, {}
    for dz in range(1, n_blk):
        where = {"blk": lax.rem(b + dz, n_blk)}
        t_copies[dz] = remote(tmpl.at[half_k], tmpl_out.at[b, half_k], tz_send.at[dz], tz_recv.at[dz], where)
        c_copies[dz] = remote(cuts, cuts_out.at[b], cz_send.at[dz], cz_recv.at[dz], where)
    for dz in range(1, n_blk):
        where = {"blk": lax.rem(b + dz, n_blk)}
        z_copies[dz] = remote(data.at[half_p], data_out.at[own, half_p], z_send.at[dz], z_recv.at[dz], where)
    x_copies, s_copies, ts_copies = {}, {}, {}
    for dx in range(1, n_det):
        x_copies[0, dx] = remote(data.at[half_p], data_out.at[own, half_p], x_send.at[0, dx], x_recv.at[0, dx],
                                 {"det": lax.rem(d + dx, n_det)})
    for dz in range(1, n_blk):
        t_copies[dz].wait_recv()
        src_b = lax.rem(b + n_blk - dz, n_blk)
        block = tmpl_out.at[src_b, half_k]
        ts_copies[dz] = remote(block, block, ts_send.at[dz], ts_recv.at[dz], {"sub": other})
    for dz in range(1, n_blk):
        z_copies[dz].wait_recv()
        src_b = lax.rem(b + n_blk - dz, n_blk)
        block = data_out.at[src_b * n_det + d, half_p]
        for dx in range(1, n_det):
            x_copies[dz, dx] = remote(block, block, x_send.at[dz, dx], x_recv.at[dz, dx],
                                      {"det": lax.rem(d + dx, n_det)})
        s_copies[dz, 0] = remote(block, block, s_send.at[dz, 0], s_recv.at[dz, 0], {"sub": other})
    for dz in range(n_blk):
        src_b = lax.rem(b + n_blk - dz, n_blk)
        for dx in range(1, n_det):
            x_copies[dz, dx].wait_recv()
            block = data_out.at[src_b * n_det + lax.rem(d + n_det - dx, n_det), half_p]
            s_copies[dz, dx] = remote(block, block, s_send.at[dz, dx], s_recv.at[dz, dx], {"sub": other})
    for copy in list(c_copies.values()) + list(ts_copies.values()) + list(s_copies.values()):
        copy.wait_recv()
    for group in (z_copies, t_copies, c_copies, x_copies, s_copies, ts_copies):
        for copy in group.values():
            copy.wait_send()
    for copy in locals_:
        copy.wait()


def gather_all(mesh_sizes, data, tmpl, cuts):
    n_blk, n_det, n_sub = mesh_sizes
    dma = pltpu.SemaphoreType.DMA
    anywhere = pl.BlockSpec(memory_space=pl.ANY)
    return pl.pallas_call(
        functools.partial(gather_kernel, n_blk, n_det, n_sub),
        out_shape=(
            jax.ShapeDtypeStruct((n_blk * n_det,) + data.shape, data.dtype),
            jax.ShapeDtypeStruct((n_blk,) + tmpl.shape, tmpl.dtype),
            jax.ShapeDtypeStruct((n_blk,) + cuts.shape, cuts.dtype),
        ),
        in_specs=[anywhere] * 3,
        out_specs=(anywhere,) * 3,
        scratch_shapes=[
            dma((3,)),
            dma((n_blk,)), dma((n_blk,)),
            dma((n_blk, n_det)), dma((n_blk, n_det)),
            dma((n_blk, n_det)), dma((n_blk, n_det)),
            dma((n_blk,)), dma((n_blk,)),
            dma((n_blk,)), dma((n_blk,)),
            dma((n_blk,)), dma((n_blk,)),
        ],
        compiler_params=pltpu.CompilerParams(collective_id=0, has_side_effects=True),
        name="gather_all",
    )(data, tmpl, cuts)


def swap_blocks(x):
    sub = lax.broadcasted_iota(jnp.int32, x.shape, 0)
    grp = lax.broadcasted_iota(jnp.int32, x.shape, 1) // NMAJ
    rows, lanes = x.shape
    for bit in (1, 2, 4):
        up = pltpu.roll(pltpu.roll(x, rows - bit, 0), NMAJ * bit, 1)
        down = pltpu.roll(pltpu.roll(x, bit, 0), lanes - NMAJ * bit, 1)
        sb, gb = (sub & bit) != 0, (grp & bit) != 0
        x = jnp.where(jnp.logical_and(jnp.logical_not(sb), gb), up,
                      jnp.where(jnp.logical_and(sb, jnp.logical_not(gb)), down, x))
    return x


def conj_product(data, tmpl):
    dr, di = data[..., :NMIN], data[..., NMIN:]
    tr, ti = tmpl[..., :NMIN], tmpl[..., NMIN:]
    return dr * tr + di * ti, di * tr - dr * ti


def compute_kernel(ids_k, ids_p, ids_t, own, data, tmpl, cuts, first, twiddle, second, tile_dft,
                   row_phase, tile_phase, peak_out, chi_out, cut_rows, cut_scr, cut_row_tab, cut_low_tab,
                   norm_tab):
    f32, bf16 = jnp.float32, jnp.bfloat16
    half = lax.axis_index("sub")
    n_tmpl = tmpl.shape[0]
    n_blk, kb, n_cut = cuts.shape
    pairs = own.shape[0]
    n_trig = chi_out.shape[0]

    cut_rows[...] = jnp.full(cut_rows.shape, NMAJ * NMIN, jnp.int32)
    for blk in range(n_blk):
        cut_rows[blk * kb:(blk + 1) * kb, 0:n_cut] = cuts[blk]
    diag = lax.broadcasted_iota(jnp.int32, (NCUT, NMIN), 0) == lax.broadcasted_iota(jnp.int32, (NCUT, NMIN), 1)
    for k in range(n_tmpl):
        line = jnp.broadcast_to(cut_rows[k:k + 1, :], (NCUT, NMIN))
        cut_scr[k * NCUT:(k + 1) * NCUT, :] = jnp.where(diag, line, 0)
    spread = jnp.ones((NMIN, NMIN), bf16)
    every = cut_scr[...]
    cut_row_tab[...] = jnp.dot((every // NMIN).astype(f32).astype(bf16), spread, preferred_element_type=f32)
    cut_low_tab[...] = jnp.dot((every % NMIN).astype(f32).astype(bf16), spread, preferred_element_type=f32)

    wide = own[...].astype(f32).reshape(pairs, NMAJ, 2 * NMIN)
    twc = jnp.broadcast_to(twiddle[:, :NMIN][None], (pairs, NMAJ, NMIN)).reshape(pairs * NMAJ, NMIN)
    tws = jnp.broadcast_to(twiddle[:, NMIN:][None], (pairs, NMAJ, NMIN)).reshape(pairs * NMAJ, NMIN)
    n_half = second.shape[1] // 2

    def one_template(k, peak):
        row = tmpl[k].astype(f32)
        norm = jnp.sum(jnp.sum(row * row, axis=0, keepdims=True), axis=1, keepdims=True)
        norm_tab[k] = jnp.broadcast_to(norm, (1, NMIN))
        real, imag = conj_product(wide, row[None])
        real = real.reshape(pairs * NMAJ, NMIN).astype(bf16)
        imag = imag.reshape(pairs * NMAJ, NMIN).astype(bf16)
        stacked = jnp.concatenate(
            [jnp.concatenate([real, imag], axis=1), jnp.concatenate([-imag, real], axis=1)], axis=0
        )
        section = jnp.dot(first[...], stacked, preferred_element_type=f32)
        sr, si = section[:, :NMIN], section[:, NMIN:]
        turned = jnp.concatenate([sr * twc - si * tws, sr * tws + si * twc], axis=1).astype(bf16)
        snr = lax.dot_general(second[half], turned, (((1,), (1,)), ((), ())), preferred_element_type=f32)
        power = snr[:n_half] * snr[:n_half] + snr[n_half:] * snr[n_half:]
        return jnp.maximum(peak, power * (1.0 / norm))

    peak = lax.fori_loop(0, n_tmpl, one_template, jnp.zeros((n_half, pairs * NMAJ), f32), unroll=4)
    swapped = swap_blocks(jnp.sqrt(peak))
    for u in range(n_half // 8):
        peak_out[:, u * 128:(u + 1) * 128] = swapped[8 * u:8 * u + 8, :]

    lane = lax.broadcasted_iota(jnp.int32, (NCUT, NMIN), 1).astype(f32)
    sub = lax.broadcasted_iota(jnp.int32, (GROUP * NCUT, NMIN), 0) % NCUT

    def one_group(q, carry):
        specs, hots, befores, lows, norms = [], [], [], [], []
        for m in range(GROUP):
            n = q * GROUP + m
            k = ids_k[0, 0, n]
            rows = data[ids_p[0, 0, n]].astype(f32)
            row = tmpl[k].astype(f32)
            real, imag = conj_product(rows, row)
            phase = tile_phase[half * (tile_phase.shape[0] // 2) + ids_t[0, 0, n]]
            pc, ps = phase[:, :NMIN], phase[:, NMIN:]
            specs.append(jnp.concatenate([real * pc - imag * ps, real * ps + imag * pc], axis=1).astype(bf16))
            at = pl.ds(pl.multiple_of(k * NCUT, NCUT), NCUT)
            cut_row = cut_row_tab[at, :]
            base = float(m * NMAJ)
            hots.append((lane == cut_row + base).astype(f32))
            befores.append(jnp.logical_and(lane >= base, lane < cut_row + base).astype(f32))
            lows.append(cut_low_tab[at, :])
            norms.append(norm_tab[k])
        z = jnp.concatenate(specs, axis=0)
        hot = jnp.concatenate(hots, axis=0)
        cut_at = jnp.concatenate(lows, axis=0)
        hot = hot.astype(bf16)
        before = jnp.concatenate(befores, axis=0).astype(bf16)
        lanes = lax.broadcasted_iota(jnp.int32, cut_at.shape, 1).astype(f32)
        keep = lanes < cut_at
        picked = jnp.dot(hot, z, preferred_element_type=f32)
        part = jnp.concatenate(
            [jnp.where(keep, picked[:, :NMIN], 0.0), jnp.where(keep, picked[:, NMIN:], 0.0)], axis=1
        ).astype(bf16)
        g = jnp.dot(part, tile_dft[...], preferred_element_type=f32)
        turn = jnp.dot(hot, row_phase[...], preferred_element_type=f32)
        f = jnp.dot(z, tile_dft[...], preferred_element_type=f32)
        own_turn = row_phase[...].astype(f32)

        def rotate(v, w):
            vr, vi, wr, wi = v[:, :NMIN], v[:, NMIN:], w[:, :NMIN], w[:, NMIN:]
            return jnp.concatenate([vr * wr - vi * wi, vr * wi + vi * wr], axis=1)

        g = rotate(g, turn)
        f = rotate(f, own_turn)
        high = f.astype(bf16)
        low = (f - high.astype(f32)).astype(bf16)
        prefix = g + jnp.dot(
            jnp.concatenate([before, before], axis=1), jnp.concatenate([high, low], axis=0),
            preferred_element_type=f32,
        )
        prev = pltpu.roll(prefix, 1, 0)
        pr, pi = prefix[:, :NMIN], prefix[:, NMIN:]
        br = pr - jnp.where(sub == 0, 0.0, prev[:, :NMIN])
        bi = pi - jnp.where(sub == 0, 0.0, prev[:, NMIN:])
        br, bi = br.reshape(GROUP, NCUT, NMIN), bi.reshape(GROUP, NCUT, NMIN)
        tr = jnp.sum(br, axis=1, keepdims=True)
        ti = jnp.sum(bi, axis=1, keepdims=True)
        dr, di = br - tr * (1.0 / NCUT), bi - ti * (1.0 / NCUT)
        spread_sq = jnp.sum(dr * dr + di * di, axis=1)
        norm = jnp.concatenate(norms, axis=0)
        reduced = spread_sq * (NCUT / (2.0 * NCUT - 2.0)) / norm
        tr, ti = tr.reshape(GROUP, NMIN), ti.reshape(GROUP, NMIN)
        rho = jnp.sqrt((tr * tr + ti * ti) / norm)
        bend = jnp.exp(jnp.log((1.0 + reduced * reduced * reduced) * 0.5) * (-1.0 / 6.0))
        chi_out[pl.ds(pl.multiple_of(q * GROUP, GROUP), GROUP), :] = jnp.where(reduced > 1.0, rho * bend, rho)
        return carry

    lax.fori_loop(0, n_trig // GROUP, one_group, 0, unroll=2)


def compute(ids_k, ids_p, ids_t, own, data, tmpl, cuts, tables):
    n_tmpl = tmpl.shape[0]
    vmem = pl.BlockSpec(memory_space=pltpu.VMEM)
    smem = pl.BlockSpec(memory_space=pltpu.SMEM)
    n_half = tables[2].shape[1] // 2
    return pl.pallas_call(
        compute_kernel,
        out_shape=(
            jax.ShapeDtypeStruct((own.shape[0], n_half * NMAJ), jnp.float32),
            jax.ShapeDtypeStruct((ids_k.shape[-1], STEPS * NMAJ), jnp.float32),
        ),
        in_specs=[smem] * 3 + [vmem] * 10,
        out_specs=(vmem, vmem),
        scratch_shapes=[
            pltpu.VMEM((n_tmpl, NMIN), jnp.int32),
            pltpu.VMEM((n_tmpl * NCUT, NMIN), jnp.int32),
            pltpu.VMEM((n_tmpl * NCUT, NMIN), jnp.float32),
            pltpu.VMEM((n_tmpl * NCUT, NMIN), jnp.float32),
            pltpu.VMEM((n_tmpl, 1, NMIN), jnp.float32),
        ],
        compiler_params=pltpu.CompilerParams(vmem_limit_bytes=48 * 1024 * 1024),
        name="filter_and_chi",
    )(ids_k, ids_p, ids_t, own, data, tmpl, cuts, *tables)


def body(sizes, data, templates, bin_cuts, trig_template, trig_pair, trig_tile):
    tables = tuple(jnp.asarray(t) for t in host_tables(sizes[2]))
    all_data, all_tmpl, all_cuts = gather_all(sizes, data, templates, bin_cuts)
    peak, chi = compute(
        trig_template, trig_pair, trig_tile, data,
        all_data.reshape((-1,) + data.shape[1:]),
        all_tmpl.reshape((-1,) + templates.shape[1:]),
        all_cuts, tables,
    )
    return peak, chi.reshape(trig_template.shape + (chi.shape[1],))


def solution(mesh):
    sizes = (mesh.shape["blk"], mesh.shape["det"], mesh.shape["sub"])
    return jax.shard_map(
        functools.partial(body, sizes),
        mesh=mesh,
        in_specs=(
            P(("groups", "blk", "det"), None, None),
            P(("groups", "blk"), None, None),
            P(("groups", "blk"), None),
            P(("groups", "blk", "det"), "sub", None),
            P(("groups", "blk", "det"), "sub", None),
            P(("groups", "blk", "det"), "sub", None),
        ),
        out_specs=(
            P(("groups", "blk", "det"), "sub"),
            P(("groups", "blk", "det"), "sub", None, None),
        ),
        check_vma=False,
    )
```

time: 168 us -> 33.7 us (0.20)
  the two profiles are of different devices: /device:TPU:0 before, /device:TPU:1 now
where the time goes in v1:
time: 33.7 us; the launch traced here: 33.2 us
  Pallas kernels  26.4 us (78%)
  local copies, waits for them, and re-layouts  6.09 us (18%)
  between operations  0.73 us (2%)
    pallas_call x1, Pallas kernels, gather_all(): pl.pallas_call(functools.partial(gather_kernel, n_blk, n_det, n_sub), out...  16.3 us
    pallas_call x1, Pallas kernels, compute(): pl.pallas_call(compute_kernel, out_shape=(jax.ShapeDtypeStruct((own.shape...  10.2 us
    unnamed x26, local copies, waits for them, and re-layouts  6.09 us

profile of v1, /device:TPU:1, one launch (start us, length us, event | category | flops | bytes accessed | tf_op | source)
XLA Modules:
  0.0 33.2 jit_solution(10159561798056792172)
XLA Ops:
  0.6 0.0 copy-start.1
  0.6 0.0 copy-start.7
  0.7 0.0 copy-start.8
  0.7 0.0 copy-start.12
  0.7 16.3 %gather_all.1 = (bf16[8,8,16,256]{3,2,1,0:T(8,128)(2,1)}, bf16[4,4,16,256]{3,2,1,0:T(8,128)(2,1)}, s32[4,4,15]{2,1,0:T(4,128)}) custom-call(bf16[8,16,256]{2,1,0:T(8,128)(2,1)} %own.1, bf16[4,16,256]{2,1,0:T(8,128)(2,1)} %tmpl.1, s32[4,15]{1,0:T(4,128)} %cuts.1), custom_call_target="tpu_custom_call" | custom-call | tf_op jit(solution)/shard_map/gather_all/pallas_call | solution.py:136
  16.9 0.0 copy-start.9
  16.9 0.0 copy-start.10
  17.0 0.0 copy-start.11
  17.0 0.0 copy-done.1
  17.0 0.0 copy-done.7
  17.0 0.0 copy-done.8
  17.0 0.0 copy-done.12
  17.0 0.6 %copy-done.9 = s32[4,4,15]{2,1,0:T(4,128)S(1)} copy-done((s32[4,4,15]{2,1,0:T(4,128)S(1)}, s32[4,4,15]{2,1,0:T(4,128)}, u32[]{:S(2)}) %copy-start.9) | copy-done | bytes 984
  17.6 0.0 copy-done.10
  17.6 0.0 copy-done.11
  17.6 0.0 copy-start
  17.6 1.0 %copy-done = bf16[8,8,16,256]{3,2,1,0:T(8,128)(2,1)S(1)} copy-done((bf16[8,8,16,256]{3,2,1,0:T(8,128)(2,1)S(1)}, bf16[8,8,16,256]{3,2,1,0:T(8,128)(2,1)}, u32[]{:S(2)}) %copy-start) | copy-done | bytes 524312
  18.7 0.0 copy-start.2
  18.7 0.9 %copy-done.2 = bf16[256,256]{1,0:T(8,128)(2,1)S(1)} copy-done((bf16[256,256]{1,0:T(8,128)(2,1)S(1)}, bf16[256,256]{1,0:T(8,128)(2,1)}, u32[]{:S(2)}) %copy-start.2) | copy-done | bytes 131096
  19.6 0.9 %copy-done.3 = bf16[2,128,256]{2,1,0:T(8,128)(2,1)S(1)} copy-done((bf16[2,128,256]{2,1,0:T(8,128)(2,1)S(1)}, bf16[2,128,256]{2,1,0:T(8,128)(2,1)}, u32[]{:S(2)}) %copy-start.3) | copy-done | bytes 131096
  20.5 0.9 %copy-done.4 = bf16[4,4,16,256]{3,2,1,0:T(8,128)(2,1)S(1)} copy-done((bf16[4,4,16,256]{3,2,1,0:T(8,128)(2,1)S(1)}, bf16[4,4,16,256]{3,2,1,0:T(8,128)(2,1)}, u32[]{:S(2)}) %copy-start.4) | copy-done | bytes 131096
  21.4 0.8 %copy-done.5 = bf16[128,256]{1,0:T(8,128)(2,1)S(1)} copy-done((bf16[128,256]{1,0:T(8,128)(2,1)S(1)}, bf16[128,256]{1,0:T(8,128)(2,1)}, u32[]{:S(2)}) %copy-start.5) | copy-done | bytes 65560
  22.2 0.8 %copy-done.6 = bf16[128,256]{1,0:T(8,128)(2,1)S(1)} copy-done((bf16[128,256]{1,0:T(8,128)(2,1)S(1)}, bf16[128,256]{1,0:T(8,128)(2,1)}, u32[]{:S(2)}) %copy-start.6) | copy-done | bytes 65560
  23.1 10.2 %filter_and_chi.1 = (f32[8,1024]{1,0:T(8,128)}, f32[128,128]{1,0:T(8,128)}) custom-call(s32[1,1,128]{2,1,0:T(1,128)S(1)} %copy-done.10, s32[1,1,128]{2,1,0:T(1,128)S(1)} %copy-done.11, s32[1,1,128]{2,1,0:T(1,128)S(1)} %copy-done.12, bf16[8,16,256]{2,1,0:T(8,128)(2,1)S(1)} %copy-done.1, bf16[64,16,256]{2,1,0:T(8,128)(2,1)S(1)} %bitcast.3, ...), custom_call_target="tpu_custom_call" | custom-call | tf_op jit(solution)/shard_map/filter_and_chi/pallas_call | solution.py:301
  (4 shorter events, 0.0 us)
Async XLA Ops:
  0.6 16.3 %copy-start.1 = (bf16[8,16,256]{2,1,0:T(8,128)(2,1)S(1)}, bf16[8,16,256]{2,1,0:T(8,128)(2,1)}, u32[]{:S(2)}) copy-start(bf16[8,16,256]{2,1,0:T(8,128)(2,1)} %own.1) | copy-start | bytes 196612
  0.6 16.3 %copy-start.7 = (f32[16,1,256]{2,1,0:T(1,128)S(1)}, f32[16,1,256]{2,1,0:T(1,128)}, u32[]{:S(2)}) copy-start(f32[16,1,256]{2,1,0:T(1,128)} %constant.17.clone.tile_phase) | copy-start | bytes 49156
  0.7 16.3 %copy-start.8 = (f32[16,256]{1,0:T(8,128)S(1)}, f32[16,256]{1,0:T(8,128)}, u32[]{:S(2)}) copy-start(f32[16,256]{1,0:T(8,128)} %constant.13.clone.twiddle) | copy-start | bytes 49156
  0.7 16.3 %copy-start.12 = (s32[1,1,128]{2,1,0:T(1,128)S(1)}, s32[1,1,128]{2,1,0:T(1,128)}, u32[]{:S(2)}) copy-start(s32[1,1,128]{2,1,0:T(1,128)} %ids_t.1) | copy-start | bytes 1540
  16.9 0.7 %copy-start.9 = (s32[4,4,15]{2,1,0:T(4,128)S(1)}, s32[4,4,15]{2,1,0:T(4,128)}, u32[]{:S(2)}) copy-start(s32[4,4,15]{2,1,0:T(4,128)} %get-tuple-element.9.cuts) | copy-start | bytes 2884
  16.9 0.7 %copy-start.10 = (s32[1,1,128]{2,1,0:T(1,128)S(1)}, s32[1,1,128]{2,1,0:T(1,128)}, u32[]{:S(2)}) copy-start(s32[1,1,128]{2,1,0:T(1,128)} %ids_k.1) | copy-start | bytes 1540
  17.0 0.7 %copy-start.11 = (s32[1,1,128]{2,1,0:T(1,128)S(1)}, s32[1,1,128]{2,1,0:T(1,128)}, u32[]{:S(2)}) copy-start(s32[1,1,128]{2,1,0:T(1,128)} %ids_p.1) | copy-start | bytes 1540
  17.6 1.0 %copy-start = (bf16[8,8,16,256]{3,2,1,0:T(8,128)(2,1)S(1)}, bf16[8,8,16,256]{3,2,1,0:T(8,128)(2,1)}, u32[]{:S(2)}) copy-start(bf16[8,8,16,256]{3,2,1,0:T(8,128)(2,1)} %get-tuple-element.7) | copy-start | bytes 1572868
  18.7 0.9 %copy-start.2 = (bf16[256,256]{1,0:T(8,128)(2,1)S(1)}, bf16[256,256]{1,0:T(8,128)(2,1)}, u32[]{:S(2)}) copy-start(bf16[256,256]{1,0:T(8,128)(2,1)} %constant.15.clone.tile_dft) | copy-start | bytes 393220
  19.6 0.9 %copy-start.3 = (bf16[2,128,256]{2,1,0:T(8,128)(2,1)S(1)}, bf16[2,128,256]{2,1,0:T(8,128)(2,1)}, u32[]{:S(2)}) copy-start(bf16[2,128,256]{2,1,0:T(8,128)(2,1)} %constant.14.clone.second) | copy-start | bytes 393220
  20.5 0.9 %copy-start.4 = (bf16[4,4,16,256]{3,2,1,0:T(8,128)(2,1)S(1)}, bf16[4,4,16,256]{3,2,1,0:T(8,128)(2,1)}, u32[]{:S(2)}) copy-start(bf16[4,4,16,256]{3,2,1,0:T(8,128)(2,1)} %get-tuple-element.8) | copy-start | bytes 393220
  21.4 0.8 %copy-start.5 = (bf16[128,256]{1,0:T(8,128)(2,1)S(1)}, bf16[128,256]{1,0:T(8,128)(2,1)}, u32[]{:S(2)}) copy-start(bf16[128,256]{1,0:T(8,128)(2,1)} %constant.16.clone.row_phase) | copy-start | bytes 196612
  22.2 0.8 %copy-start.6 = (bf16[128,256]{1,0:T(8,128)(2,1)S(1)}, bf16[128,256]{1,0:T(8,128)(2,1)}, u32[]{:S(2)}) copy-start(bf16[128,256]{1,0:T(8,128)(2,1)} %constant.12.clone.first) | copy-start | bytes 196612

commit v2 on v1

v2 whole, which is shorter than its diff:
```python
import functools
import math

import jax
import jax.numpy as jnp
import numpy as np
from jax import lax
from jax.experimental import pallas as pl
from jax.experimental.pallas import tpu as pltpu
from jax.sharding import PartitionSpec as P

MESH = pl.DeviceIdType.MESH
NMAJ = 16
NMIN = 128
NCUT = 16
STEPS = 8
GROUP = 8


def unit_circle(index, period):
    angle = (index % period) * (2.0 * math.pi / period)
    return np.cos(angle), np.sin(angle)


def host_tables(n_sub):
    bf16 = jnp.bfloat16
    major = np.arange(NMAJ)
    minor = np.arange(NMIN)
    cos16, sin16 = unit_circle(major[:, None] * major[None, :], NMAJ)
    eye = np.eye(GROUP)
    first = np.concatenate([np.kron(eye, cos16), np.kron(eye, sin16)], axis=1).astype(bf16)
    twc, tws = unit_circle(major[:, None] * minor[None, :], NMAJ * NMIN)
    twiddle = np.concatenate([twc, tws], axis=1).astype(np.float32)
    n_half = NMIN // n_sub
    second = []
    for half in range(n_sub):
        steps = half * n_half + np.arange(n_half)
        cosine, sine = unit_circle(steps[:, None] * minor[None, :], NMIN)
        real_rows = np.concatenate([cosine, -sine], axis=1)
        imag_rows = np.concatenate([sine, cosine], axis=1)
        second.append(np.concatenate([real_rows, imag_rows], axis=0))
    second = np.stack(second).astype(bf16)
    times = np.arange(NMAJ * STEPS)
    cosine, sine = unit_circle(minor[:, None] * times[None, :], NMAJ * NMIN)
    tile_dft = np.concatenate(
        [np.concatenate([cosine, sine], axis=1), np.concatenate([-sine, cosine], axis=1)], axis=0
    ).astype(bf16)
    rowc, rows = unit_circle(major[:, None] * (times % NMAJ)[None, :], NMAJ)
    row_phase = np.tile(np.concatenate([rowc, rows], axis=1), (GROUP, 1)).astype(bf16)
    starts = np.arange(NMIN // STEPS) * STEPS
    phc, phs = unit_circle(starts[:, None] * minor[None, :], NMIN)
    tile_phase = np.concatenate([phc, phs], axis=1).astype(np.float32)[:, None, :]
    return first, twiddle, second, tile_dft, row_phase, tile_phase


def swap_blocks(x):
    sub = lax.broadcasted_iota(jnp.int32, x.shape, 0)
    grp = lax.broadcasted_iota(jnp.int32, x.shape, 1) // NMAJ
    rows, lanes = x.shape
    for bit in (1, 2, 4):
        up = pltpu.roll(pltpu.roll(x, rows - bit, 0), NMAJ * bit, 1)
        down = pltpu.roll(pltpu.roll(x, bit, 0), lanes - NMAJ * bit, 1)
        sb, gb = (sub & bit) != 0, (grp & bit) != 0
        x = jnp.where(jnp.logical_and(jnp.logical_not(sb), gb), up,
                      jnp.where(jnp.logical_and(sb, jnp.logical_not(gb)), down, x))
    return x


def conj_product(data, tmpl):
    dr, di = data[..., :NMIN], data[..., NMIN:]
    tr, ti = tmpl[..., :NMIN], tmpl[..., NMIN:]
    return dr * tr + di * ti, di * tr - dr * ti


def fused_kernel(n_blk, n_det, n_sub, *refs):
    (ids_k_in, ids_p_in, ids_t_in, own_in, tmpl_in, cuts_in, first_in, twiddle_in, second_in, tile_dft_in,
     row_phase_in, tile_phase_in, peak_out, chi_out, data4, tmpl4, cuts, ids_k, ids_p, ids_t, first, twiddle,
     second, tile_dft, row_phase, tile_phase, cut_rows, cut_scr, cut_row_tab, cut_low_tab, norm_tab,
     local_sem, z_send, z_recv, x_send, x_recv, s_send, s_recv, tz_send, tz_recv, ts_send, ts_recv,
     cz_send, cz_recv) = refs
    f32, bf16 = jnp.float32, jnp.bfloat16
    b = lax.axis_index("blk")
    d = lax.axis_index("det")
    half = lax.axis_index("sub")
    other = n_sub - 1 - half
    pairs = own_in.shape[0]
    kb = tmpl_in.shape[0]
    n_cut = cuts_in.shape[1]
    n_tmpl = n_blk * kb
    n_trig = chi_out.shape[0]
    hp, hk = pairs // n_sub, kb // n_sub
    own = b * n_det + d

    barrier = pltpu.get_barrier_semaphore()
    for dz in range(1, n_blk):
        pl.semaphore_signal(barrier, inc=1, device_id={"blk": lax.rem(b + dz, n_blk)}, device_id_type=MESH)
    for dx in range(1, n_det):
        pl.semaphore_signal(barrier, inc=1, device_id={"det": lax.rem(d + dx, n_det)}, device_id_type=MESH)
    pl.semaphore_signal(barrier, inc=1, device_id={"sub": other}, device_id_type=MESH)

    moves = [(tmpl_in, tmpl4.at[pl.ds(b * kb, kb)]), (own_in, data4.at[pl.ds(own * pairs, pairs)]), (cuts_in, cuts.at[b]), (first_in, first),
             (twiddle_in, twiddle), (second_in.at[half], second), (tile_dft_in, tile_dft), (row_phase_in, row_phase),
             (tile_phase_in, tile_phase), (ids_k_in, ids_k), (ids_p_in, ids_p), (ids_t_in, ids_t)]
    fetches = [pltpu.make_async_copy(src, dst, local_sem.at[i]) for i, (src, dst) in enumerate(moves)]
    for copy in fetches:
        copy.start()
    for copy in fetches[:3]:
        copy.wait()
    pl.semaphore_wait(barrier, n_blk + n_det - 1)

    def remote(ref, send, recv, where):
        copy = pltpu.make_async_remote_copy(src_ref=ref, dst_ref=ref, send_sem=send, recv_sem=recv,
                                            device_id=where, device_id_type=MESH)
        copy.start()
        return copy

    def data_half(place):
        return data4.at[pl.ds(place * pairs + half * hp, hp)]

    def tmpl_half(place):
        return tmpl4.at[pl.ds(place * kb + half * hk, hk)]

    z_copies, t_copies, c_copies, x_copies, s_copies, ts_copies = {}, {}, {}, {}, {}, {}
    for dz in range(1, n_blk):
        where = {"blk": lax.rem(b + dz, n_blk)}
        t_copies[dz] = remote(tmpl_half(b), tz_send.at[dz], tz_recv.at[dz], where)
        c_copies[dz] = remote(cuts.at[b], cz_send.at[dz], cz_recv.at[dz], where)
    for dz in range(1, n_blk):
        where = {"blk": lax.rem(b + dz, n_blk)}
        z_copies[dz] = remote(data_half(own), z_send.at[dz], z_recv.at[dz], where)
    for dx in range(1, n_det):
        x_copies[0, dx] = remote(data_half(own), x_send.at[0, dx], x_recv.at[0, dx],
                                 {"det": lax.rem(d + dx, n_det)})
    for copy in fetches[3:]:
        copy.wait()

    wide = data4[pl.ds(own * pairs, pairs)].astype(f32)
    twc = jnp.broadcast_to(twiddle[:, :NMIN][None], (pairs, NMAJ, NMIN)).reshape(pairs * NMAJ, NMIN)
    tws = jnp.broadcast_to(twiddle[:, NMIN:][None], (pairs, NMAJ, NMIN)).reshape(pairs * NMAJ, NMIN)
    n_half = second.shape[0] // 2

    def peak_of(src_b, peak):
        def one_template(k, peak):
            row = tmpl4[src_b * kb + k].astype(f32)
            norm = jnp.sum(jnp.sum(row * row, axis=0, keepdims=True), axis=1, keepdims=True)
            norm_tab[src_b * kb + k] = jnp.broadcast_to(norm, (1, NMIN))
            real, imag = conj_product(wide, row[None])
            real = real.reshape(pairs * NMAJ, NMIN).astype(bf16)
            imag = imag.reshape(pairs * NMAJ, NMIN).astype(bf16)
            stacked = jnp.concatenate(
                [jnp.concatenate([real, imag], axis=1), jnp.concatenate([-imag, real], axis=1)], axis=0
            )
            section = jnp.dot(first[...], stacked, preferred_element_type=f32)
            sr, si = section[:, :NMIN], section[:, NMIN:]
            turned = jnp.concatenate([sr * twc - si * tws, sr * tws + si * twc], axis=1).astype(bf16)
            snr = lax.dot_general(second[...], turned, (((1,), (1,)), ((), ())), preferred_element_type=f32)
            power = snr[:n_half] * snr[:n_half] + snr[n_half:] * snr[n_half:]
            return jnp.maximum(peak, power * (1.0 / norm))

        return lax.fori_loop(0, kb, one_template, peak, unroll=True)

    peak = peak_of(b, jnp.zeros((n_half, pairs * NMAJ), f32))
    for dz in range(1, n_blk):
        t_copies[dz].wait_recv()
        src_b = lax.rem(b + n_blk - dz, n_blk)
        ts_copies[dz] = remote(tmpl_half(src_b), ts_send.at[dz], ts_recv.at[dz], {"sub": other})
    for dz in range(1, n_blk):
        z_copies[dz].wait_recv()
        src_b = lax.rem(b + n_blk - dz, n_blk)
        block = data_half(src_b * n_det + d)
        for dx in range(1, n_det):
            x_copies[dz, dx] = remote(block, x_send.at[dz, dx], x_recv.at[dz, dx],
                                      {"det": lax.rem(d + dx, n_det)})
        s_copies[dz, 0] = remote(block, s_send.at[dz, 0], s_recv.at[dz, 0], {"sub": other})
        ts_copies[dz].wait_recv()
        peak = peak_of(src_b, peak)

    for copy in c_copies.values():
        copy.wait_recv()
    cut_rows[...] = jnp.full(cut_rows.shape, NMAJ * NMIN, jnp.int32)
    for blk in range(n_blk):
        cut_rows[blk * kb:(blk + 1) * kb, 0:n_cut] = cuts[blk]
    diag = lax.broadcasted_iota(jnp.int32, (NCUT, NMIN), 0) == lax.broadcasted_iota(jnp.int32, (NCUT, NMIN), 1)
    for k in range(n_tmpl):
        line = jnp.broadcast_to(cut_rows[k:k + 1, :], (NCUT, NMIN))
        cut_scr[k * NCUT:(k + 1) * NCUT, :] = jnp.where(diag, line, 0)
    spread = jnp.ones((NMIN, NMIN), bf16)
    every = cut_scr[...]
    cut_row_tab[...] = jnp.dot(
        (every >> 7).astype(f32).astype(bf16), spread, preferred_element_type=f32
    ).reshape(n_tmpl, NCUT, NMIN)
    cut_low_tab[...] = jnp.dot(
        (every & (NMIN - 1)).astype(f32).astype(bf16), spread, preferred_element_type=f32
    ).reshape(n_tmpl, NCUT, NMIN)

    for dz in range(n_blk):
        src_b = lax.rem(b + n_blk - dz, n_blk)
        for dx in range(1, n_det):
            x_copies[dz, dx].wait_recv()
            block = data_half(src_b * n_det + lax.rem(d + n_det - dx, n_det))
            s_copies[dz, dx] = remote(block, s_send.at[dz, dx], s_recv.at[dz, dx], {"sub": other})

    swapped = swap_blocks(jnp.sqrt(peak))
    for u in range(n_half // 8):
        peak_out[:, u * 128:(u + 1) * 128] = swapped[8 * u:8 * u + 8, :]
    for copy in s_copies.values():
        copy.wait_recv()

    lane = lax.broadcasted_iota(jnp.int32, (NCUT, NMIN), 1).astype(f32)
    sub = lax.broadcasted_iota(jnp.int32, (GROUP * NCUT, NMIN), 0) % NCUT

    def one_group(q, carry):
        specs, hots, befores, lows, norms = [], [], [], [], []
        for m in range(GROUP):
            n = q * GROUP + m
            k = ids_k[0, 0, n]
            rows = data4[ids_p[0, 0, n]].astype(f32)
            row = tmpl4[k].astype(f32)
            real, imag = conj_product(rows, row)
            phase = tile_phase[half * (tile_phase.shape[0] // 2) + ids_t[0, 0, n]]
            pc, ps = phase[:, :NMIN], phase[:, NMIN:]
            specs.append(jnp.concatenate([real * pc - imag * ps, real * ps + imag * pc], axis=1).astype(bf16))
            cut_row = cut_row_tab[k]
            base = float(m * NMAJ)
            hots.append((lane == cut_row + base).astype(f32))
            befores.append(jnp.logical_and(lane >= base, lane < cut_row + base).astype(f32))
            lows.append(cut_low_tab[k])
            norms.append(norm_tab[k])
        z = jnp.concatenate(specs, axis=0)
        hot = jnp.concatenate(hots, axis=0)
        cut_at = jnp.concatenate(lows, axis=0)
        hot = hot.astype(bf16)
        before = jnp.concatenate(befores, axis=0).astype(bf16)
        lanes = lax.broadcasted_iota(jnp.int32, cut_at.shape, 1).astype(f32)
        keep = lanes < cut_at
        picked = jnp.dot(hot, z, preferred_element_type=f32)
        part = jnp.concatenate(
            [jnp.where(keep, picked[:, :NMIN], 0.0), jnp.where(keep, picked[:, NMIN:], 0.0)], axis=1
        ).astype(bf16)
        g = jnp.dot(part, tile_dft[...], preferred_element_type=f32)
        turn = jnp.dot(hot, row_phase[...], preferred_element_type=f32)
        f = jnp.dot(z, tile_dft[...], preferred_element_type=f32)
        own_turn = row_phase[...].astype(f32)

        def rotate(v, w):
            vr, vi, wr, wi = v[:, :NMIN], v[:, NMIN:], w[:, :NMIN], w[:, NMIN:]
            return jnp.concatenate([vr * wr - vi * wi, vr * wi + vi * wr], axis=1)

        g = rotate(g, turn)
        f = rotate(f, own_turn)
        high = f.astype(bf16)
        low = (f - high.astype(f32)).astype(bf16)
        prefix = g + jnp.dot(
            jnp.concatenate([before, before], axis=1), jnp.concatenate([high, low], axis=0),
            preferred_element_type=f32,
        )
        prev = pltpu.roll(prefix, 1, 0)
        pr, pi = prefix[:, :NMIN], prefix[:, NMIN:]
        br = pr - jnp.where(sub == 0, 0.0, prev[:, :NMIN])
        bi = pi - jnp.where(sub == 0, 0.0, prev[:, NMIN:])
        br, bi = br.reshape(GROUP, NCUT, NMIN), bi.reshape(GROUP, NCUT, NMIN)
        tr = jnp.sum(br, axis=1, keepdims=True)
        ti = jnp.sum(bi, axis=1, keepdims=True)
        dr, di = br - tr * (1.0 / NCUT), bi - ti * (1.0 / NCUT)
        spread_sq = jnp.sum(dr * dr + di * di, axis=1)
        norm = jnp.concatenate(norms, axis=0)
        reduced = spread_sq * (NCUT / (2.0 * NCUT - 2.0)) / norm
        tr, ti = tr.reshape(GROUP, NMIN), ti.reshape(GROUP, NMIN)
        rho = jnp.sqrt((tr * tr + ti * ti) / norm)
        bend = jnp.exp(jnp.log((1.0 + reduced * reduced * reduced) * 0.5) * (-1.0 / 6.0))
        chi_out[pl.ds(pl.multiple_of(q * GROUP, GROUP), GROUP), :] = jnp.where(reduced > 1.0, rho * bend, rho)
        return carry

    lax.fori_loop(0, n_trig // GROUP, one_group, 0, unroll=2)

    for group in (z_copies, t_copies, c_copies, x_copies, s_copies, ts_copies):
        for copy in group.values():
            copy.wait_send()


def fused(sizes, ids_k, ids_p, ids_t, own, tmpl, cuts, tables):
    n_blk, n_det, n_sub = sizes
    n_tmpl = n_blk * tmpl.shape[0]
    anywhere = pl.BlockSpec(memory_space=pl.ANY)
    vmem = pl.BlockSpec(memory_space=pltpu.VMEM)
    dma = pltpu.SemaphoreType.DMA
    n_half = tables[2].shape[1] // 2
    scratch = [
        pltpu.VMEM((n_blk * n_det * own.shape[0],) + own.shape[1:], own.dtype),
        pltpu.VMEM((n_tmpl,) + tmpl.shape[1:], tmpl.dtype),
        pltpu.VMEM((n_blk,) + cuts.shape, cuts.dtype),
    ]
    scratch += [pltpu.SMEM(ids_k.shape, jnp.int32)] * 3
    for i, table in enumerate(tables):
        scratch.append(pltpu.VMEM(table.shape[1:] if i == 2 else table.shape, table.dtype))
    scratch += [
        pltpu.VMEM((n_tmpl, NMIN), jnp.int32),
        pltpu.VMEM((n_tmpl * NCUT, NMIN), jnp.int32),
        pltpu.VMEM((n_tmpl, NCUT, NMIN), jnp.float32),
        pltpu.VMEM((n_tmpl, NCUT, NMIN), jnp.float32),
        pltpu.VMEM((n_tmpl, 1, NMIN), jnp.float32),
        dma((12,)),
        dma((n_blk,)), dma((n_blk,)),
        dma((n_blk, n_det)), dma((n_blk, n_det)),
        dma((n_blk, n_det)), dma((n_blk, n_det)),
        dma((n_blk,)), dma((n_blk,)),
        dma((n_blk,)), dma((n_blk,)),
        dma((n_blk,)), dma((n_blk,)),
    ]
    return pl.pallas_call(
        functools.partial(fused_kernel, n_blk, n_det, n_sub),
        out_shape=(
            jax.ShapeDtypeStruct((own.shape[0], n_half * NMAJ), jnp.float32),
            jax.ShapeDtypeStruct((ids_k.shape[-1], STEPS * NMAJ), jnp.float32),
        ),
        in_specs=[anywhere] * 12,
        out_specs=(vmem, vmem),
        scratch_shapes=scratch,
        compiler_params=pltpu.CompilerParams(
            collective_id=0, has_side_effects=True, vmem_limit_bytes=60 * 1024 * 1024
        ),
        name="filter_and_chi",
    )(ids_k, ids_p, ids_t, own, tmpl, cuts, *tables)


def body(sizes, data, templates, bin_cuts, trig_template, trig_pair, trig_tile):
    tables = tuple(jnp.asarray(t) for t in host_tables(sizes[2]))
    peak, chi = fused(sizes, trig_template, trig_pair, trig_tile, data, templates, bin_cuts, tables)
    return peak, chi.reshape(trig_template.shape + (chi.shape[1],))


def solution(mesh):
    sizes = (mesh.shape["blk"], mesh.shape["det"], mesh.shape["sub"])
    return jax.shard_map(
        functools.partial(body, sizes),
        mesh=mesh,
        in_specs=(
            P(("groups", "blk", "det"), None, None),
            P(("groups", "blk"), None, None),
            P(("groups", "blk"), None),
            P(("groups", "blk", "det"), "sub", None),
            P(("groups", "blk", "det"), "sub", None),
            P(("groups", "blk", "det"), "sub", None),
        ),
        out_specs=(
            P(("groups", "blk", "det"), "sub"),
            P(("groups", "blk", "det"), "sub", None, None),
        ),
        check_vma=False,
    )
```

time: 33.7 us -> 25.6 us (0.76)
  local copies, waits for them, and re-layouts: 6.09 us -> 2.04 us
  Pallas kernels: 26.4 us -> 22.7 us
    unnamed x26 -> x4, local copies, waits for them, and re-layouts: 6.09 us -> 2.04 us
    pallas_call x2 -> x1, Pallas kernels: 26.4 us -> 22.7 us  [fused(): pl.pallas_call(functools.partial(fused_kernel, n_blk, n_det, n_sub), out_...]
where the time goes in v2:
time: 25.6 us; the launch traced here: 25.4 us
  Pallas kernels  22.7 us (89%)
  local copies, waits for them, and re-layouts  2.04 us (8%)
  between operations  0.65 us (3%)
    pallas_call x1, Pallas kernels, fused(): pl.pallas_call(functools.partial(fused_kernel, n_blk, n_det, n_sub), out_...  22.7 us
    unnamed x4, local copies, waits for them, and re-layouts  2.04 us

profile of v2, /device:TPU:1, one launch (start us, length us, event | category | flops | bytes accessed | tf_op | source)
XLA Modules:
  0.0 25.4 jit_solution(14559079435289970579)
XLA Ops:
  0.6 22.7 %filter_and_chi.1 = (f32[8,1024]{1,0:T(8,128)}, f32[128,128]{1,0:T(8,128)}) custom-call(s32[1,1,128]{2,1,0:T(1,128)} %refs_0_.1, s32[1,1,128]{2,1,0:T(1,128)} %refs_1_.1, s32[1,1,128]{2,1,0:T(1,128)} %refs_2_.1, bf16[8,16,256]{2,1,0:T(8,128)(2,1)} %refs_3_.1, bf16[4,16,256]{2,1,0:T(8,128)(2,1)} %refs_4_.1, s32[4,15]{1,0:T(4,128)} %refs_5_.1, ...), custom_call_target="tpu_custom_call" | custom-call | tf_op jit(solution)/shard_map/filter_and_chi/pallas_call | solution.py:310
  23.4 0.0 copy-start
  23.4 1.4 %copy.16 = f32[8,1024]{1,0:T(8,128)} copy(f32[8,1024]{1,0:T(8,128)} %get-tuple-element.8) | data formatting | bytes 65536
  24.8 0.0 copy-done
  24.8 0.6 %copy.17 = f32[1,1,128,128]{3,2,1,0:T(8,128)} copy(f32[1,1,128,128]{3,2,1,0:T(8,128)S(1)} %bitcast.1) | data formatting | bytes 131072
Async XLA Ops:
  23.4 1.4 %copy-start = (f32[128,128]{1,0:T(8,128)S(1)}, f32[128,128]{1,0:T(8,128)}, u32[]{:S(2)}) copy-start(f32[128,128]{1,0:T(8,128)} %get-tuple-element.5) | copy-start | bytes 196612

commit v3 on v2

--- a/solution.py
+++ b/solution.py
@@ -76,6 +76,7 @@
     (ids_k_in, ids_p_in, ids_t_in, own_in, tmpl_in, cuts_in, first_in, twiddle_in, second_in, tile_dft_in,
      row_phase_in, tile_phase_in, peak_out, chi_out, data4, tmpl4, cuts, ids_k, ids_p, ids_t, first, twiddle,
      second, tile_dft, row_phase, tile_phase, cut_rows, cut_scr, cut_row_tab, cut_low_tab, norm_tab,
+     turn_tab, turned, hot_tab, before_tab, low_tab, spin_tab, scale_tab,
      local_sem, z_send, z_recv, x_send, x_recv, s_send, s_recv, tz_send, tz_recv, ts_send, ts_recv,
      cz_send, cz_recv) = refs
     f32, bf16 = jnp.float32, jnp.bfloat16
@@ -87,7 +88,7 @@
     kb = tmpl_in.shape[0]
     n_cut = cuts_in.shape[1]
     n_tmpl = n_blk * kb
-    n_trig = chi_out.shape[0]
+    n_trig = chi_out.shape[2]
     hp, hk = pairs // n_sub, kb // n_sub
     own = b * n_det + d
 
@@ -114,6 +115,15 @@
         copy.start()
         return copy
 
+    def partner(step):
+        index = b
+        bit = 1
+        while bit <= step:
+            if step & bit:
+                index = index + bit * (1 - 2 * lax.rem(b // bit, 2))
+            bit *= 2
+        return index
+
     def data_half(place):
         return data4.at[pl.ds(place * pairs + half * hp, hp)]
 
@@ -121,12 +131,12 @@
         return tmpl4.at[pl.ds(place * kb + half * hk, hk)]
 
     z_copies, t_copies, c_copies, x_copies, s_copies, ts_copies = {}, {}, {}, {}, {}, {}
-    for dz in range(1, n_blk):
-        where = {"blk": lax.rem(b + dz, n_blk)}
+    for dz in range(n_blk - 1, 0, -1):
+        where = {"blk": partner(dz)}
         t_copies[dz] = remote(tmpl_half(b), tz_send.at[dz], tz_recv.at[dz], where)
         c_copies[dz] = remote(cuts.at[b], cz_send.at[dz], cz_recv.at[dz], where)
-    for dz in range(1, n_blk):
-        where = {"blk": lax.rem(b + dz, n_blk)}
+    for dz in range(n_blk - 1, 0, -1):
+        where = {"blk": partner(dz)}
         z_copies[dz] = remote(data_half(own), z_send.at[dz], z_recv.at[dz], where)
     for dx in range(1, n_det):
         x_copies[0, dx] = remote(data_half(own), x_send.at[0, dx], x_recv.at[0, dx],
@@ -152,21 +162,21 @@
             )
             section = jnp.dot(first[...], stacked, preferred_element_type=f32)
             sr, si = section[:, :NMIN], section[:, NMIN:]
-            turned = jnp.concatenate([sr * twc - si * tws, sr * tws + si * twc], axis=1).astype(bf16)
-            snr = lax.dot_general(second[...], turned, (((1,), (1,)), ((), ())), preferred_element_type=f32)
+            bent = jnp.concatenate([sr * twc - si * tws, sr * tws + si * twc], axis=1).astype(bf16)
+            snr = lax.dot_general(second[...], bent, (((1,), (1,)), ((), ())), preferred_element_type=f32)
             power = snr[:n_half] * snr[:n_half] + snr[n_half:] * snr[n_half:]
             return jnp.maximum(peak, power * (1.0 / norm))
 
         return lax.fori_loop(0, kb, one_template, peak, unroll=True)
 
     peak = peak_of(b, jnp.zeros((n_half, pairs * NMAJ), f32))
-    for dz in range(1, n_blk):
+    for dz in range(n_blk - 1, 0, -1):
         t_copies[dz].wait_recv()
-        src_b = lax.rem(b + n_blk - dz, n_blk)
+        src_b = partner(dz)
         ts_copies[dz] = remote(tmpl_half(src_b), ts_send.at[dz], ts_recv.at[dz], {"sub": other})
-    for dz in range(1, n_blk):
+    for dz in range(n_blk - 1, 0, -1):
         z_copies[dz].wait_recv()
-        src_b = lax.rem(b + n_blk - dz, n_blk)
+        src_b = partner(dz)
         block = data_half(src_b * n_det + d)
         for dx in range(1, n_det):
             x_copies[dz, dx] = remote(block, x_send.at[dz, dx], x_recv.at[dz, dx],
@@ -193,8 +203,36 @@
         (every & (NMIN - 1)).astype(f32).astype(bf16), spread, preferred_element_type=f32
     ).reshape(n_tmpl, NCUT, NMIN)
 
-    for dz in range(n_blk):
-        src_b = lax.rem(b + n_blk - dz, n_blk)
+    lane = lax.broadcasted_iota(jnp.int32, (NCUT, NMIN), 1).astype(f32)
+    for k in range(n_tmpl * NCUT // NMIN):
+        rows = slice(k * (NMIN // NCUT), (k + 1) * (NMIN // NCUT))
+        row_at = cut_row_tab[rows].reshape(NMIN, NMIN)
+        lanes = lax.broadcasted_iota(jnp.int32, (NMIN, NMIN), 1).astype(f32)
+        turn = jnp.dot((lanes == row_at).astype(f32).astype(bf16), row_phase[...], preferred_element_type=f32)
+        turn_tab[rows] = turn.reshape(NMIN // NCUT, NCUT, 2 * NMIN)
+
+    def prepare(n, carry):
+        k = ids_k[0, 0, n]
+        row = tmpl4[k].astype(f32)
+        phase = tile_phase[half * (tile_phase.shape[0] // n_sub) + ids_t[0, 0, n]]
+        pc, ps = phase[:, :NMIN], phase[:, NMIN:]
+        tr, ti = row[:, :NMIN], row[:, NMIN:]
+        turned[n, :, :NMIN] = tr * pc + ti * ps
+        turned[n, :, NMIN:] = tr * ps - ti * pc
+        base = (lax.rem(n, GROUP) * NMAJ).astype(f32)
+        cut_row = cut_row_tab[k] + base
+        hot_tab[n] = (lane == cut_row).astype(f32).astype(bf16)
+        before_tab[n] = jnp.logical_and(lane >= base, lane < cut_row).astype(f32).astype(bf16)
+        low_tab[n] = cut_low_tab[k]
+        spin_tab[n] = turn_tab[k]
+        scale_tab[n] = norm_tab[k]
+        return carry
+
+    order = [0] + list(range(n_blk - 1, 0, -1))
+    bounds = [n_trig * i // n_blk for i in range(n_blk + 1)]
+    for turn_at, dz in enumerate(order):
+        lax.fori_loop(bounds[turn_at], bounds[turn_at + 1], prepare, 0, unroll=8)
+        src_b = partner(dz)
         for dx in range(1, n_det):
             x_copies[dz, dx].wait_recv()
             block = data_half(src_b * n_det + lax.rem(d + n_det - dx, n_det))
@@ -206,31 +244,22 @@
     for copy in s_copies.values():
         copy.wait_recv()
 
-    lane = lax.broadcasted_iota(jnp.int32, (NCUT, NMIN), 1).astype(f32)
     sub = lax.broadcasted_iota(jnp.int32, (GROUP * NCUT, NMIN), 0) % NCUT
 
     def one_group(q, carry):
-        specs, hots, befores, lows, norms = [], [], [], [], []
+        group = pl.ds(q * GROUP, GROUP)
+        specs = []
         for m in range(GROUP):
             n = q * GROUP + m
-            k = ids_k[0, 0, n]
             rows = data4[ids_p[0, 0, n]].astype(f32)
-            row = tmpl4[k].astype(f32)
-            real, imag = conj_product(rows, row)
-            phase = tile_phase[half * (tile_phase.shape[0] // 2) + ids_t[0, 0, n]]
-            pc, ps = phase[:, :NMIN], phase[:, NMIN:]
-            specs.append(jnp.concatenate([real * pc - imag * ps, real * ps + imag * pc], axis=1).astype(bf16))
-            cut_row = cut_row_tab[k]
-            base = float(m * NMAJ)
-            hots.append((lane == cut_row + base).astype(f32))
-            befores.append(jnp.logical_and(lane >= base, lane < cut_row + base).astype(f32))
-            lows.append(cut_low_tab[k])
-            norms.append(norm_tab[k])
+            dr, di = rows[:, :NMIN], rows[:, NMIN:]
+            wr, wi = turned[n, :, :NMIN], turned[n, :, NMIN:]
+            specs.append(jnp.concatenate([dr * wr - di * wi, dr * wi + di * wr], axis=1).astype(bf16))
         z = jnp.concatenate(specs, axis=0)
-        hot = jnp.concatenate(hots, axis=0)
-        cut_at = jnp.concatenate(lows, axis=0)
-        hot = hot.astype(bf16)
-        before = jnp.concatenate(befores, axis=0).astype(bf16)
+        hot = hot_tab[group].reshape(GROUP * NCUT, NMIN)
+        before = before_tab[group].reshape(GROUP * NCUT, NMIN)
+        cut_at = low_tab[group].reshape(GROUP * NCUT, NMIN)
+        turn = spin_tab[group].reshape(GROUP * NCUT, 2 * NMIN)
         lanes = lax.broadcasted_iota(jnp.int32, cut_at.shape, 1).astype(f32)
         keep = lanes < cut_at
         picked = jnp.dot(hot, z, preferred_element_type=f32)
@@ -238,7 +267,6 @@
             [jnp.where(keep, picked[:, :NMIN], 0.0), jnp.where(keep, picked[:, NMIN:], 0.0)], axis=1
         ).astype(bf16)
         g = jnp.dot(part, tile_dft[...], preferred_element_type=f32)
-        turn = jnp.dot(hot, row_phase[...], preferred_element_type=f32)
         f = jnp.dot(z, tile_dft[...], preferred_element_type=f32)
         own_turn = row_phase[...].astype(f32)
 
@@ -263,15 +291,15 @@
         ti = jnp.sum(bi, axis=1, keepdims=True)
         dr, di = br - tr * (1.0 / NCUT), bi - ti * (1.0 / NCUT)
         spread_sq = jnp.sum(dr * dr + di * di, axis=1)
-        norm = jnp.concatenate(norms, axis=0)
+        norm = scale_tab[group].reshape(GROUP, NMIN)
         reduced = spread_sq * (NCUT / (2.0 * NCUT - 2.0)) / norm
         tr, ti = tr.reshape(GROUP, NMIN), ti.reshape(GROUP, NMIN)
         rho = jnp.sqrt((tr * tr + ti * ti) / norm)
         bend = jnp.exp(jnp.log((1.0 + reduced * reduced * reduced) * 0.5) * (-1.0 / 6.0))
-        chi_out[pl.ds(pl.multiple_of(q * GROUP, GROUP), GROUP), :] = jnp.where(reduced > 1.0, rho * bend, rho)
+        chi_out[0, 0, pl.ds(pl.multiple_of(q * GROUP, GROUP), GROUP), :] = jnp.where(reduced > 1.0, rho * bend, rho)
         return carry
 
-    lax.fori_loop(0, n_trig // GROUP, one_group, 0, unroll=2)
+    lax.fori_loop(0, n_trig // GROUP, one_group, 0, unroll=8)
 
     for group in (z_copies, t_copies, c_copies, x_copies, s_copies, ts_copies):
         for copy in group.values():
@@ -281,6 +309,7 @@
 def fused(sizes, ids_k, ids_p, ids_t, own, tmpl, cuts, tables):
     n_blk, n_det, n_sub = sizes
     n_tmpl = n_blk * tmpl.shape[0]
+    n_trig = ids_k.shape[-1]
     anywhere = pl.BlockSpec(memory_space=pl.ANY)
     vmem = pl.BlockSpec(memory_space=pltpu.VMEM)
     dma = pltpu.SemaphoreType.DMA
@@ -299,6 +328,13 @@
         pltpu.VMEM((n_tmpl, NCUT, NMIN), jnp.float32),
         pltpu.VMEM((n_tmpl, NCUT, NMIN), jnp.float32),
         pltpu.VMEM((n_tmpl, 1, NMIN), jnp.float32),
+        pltpu.VMEM((n_tmpl, NCUT, 2 * NMIN), jnp.float32),
+        pltpu.VMEM((n_trig, NMAJ, 2 * NMIN), jnp.float32),
+        pltpu.VMEM((n_trig, NCUT, NMIN), jnp.bfloat16),
+        pltpu.VMEM((n_trig, NCUT, NMIN), jnp.bfloat16),
+        pltpu.VMEM((n_trig, NCUT, NMIN), jnp.float32),
+        pltpu.VMEM((n_trig, NCUT, 2 * NMIN), jnp.float32),
+        pltpu.VMEM((n_trig, 1, NMIN), jnp.float32),
         dma((12,)),
         dma((n_blk,)), dma((n_blk,)),
         dma((n_blk, n_det)), dma((n_blk, n_det)),
@@ -311,7 +347,7 @@
         functools.partial(fused_kernel, n_blk, n_det, n_sub),
         out_shape=(
             jax.ShapeDtypeStruct((own.shape[0], n_half * NMAJ), jnp.float32),
-            jax.ShapeDtypeStruct((ids_k.shape[-1], STEPS * NMAJ), jnp.float32),
+            jax.ShapeDtypeStruct(ids_k.shape + (STEPS * NMAJ,), jnp.float32),
         ),
         in_specs=[anywhere] * 12,
         out_specs=(vmem, vmem),
@@ -326,7 +362,7 @@
 def body(sizes, data, templates, bin_cuts, trig_template, trig_pair, trig_tile):
     tables = tuple(jnp.asarray(t) for t in host_tables(sizes[2]))
     peak, chi = fused(sizes, trig_template, trig_pair, trig_tile, data, templates, bin_cuts, tables)
-    return peak, chi.reshape(trig_template.shape + (chi.shape[1],))
+    return peak, chi
 
 
 def solution(mesh):

time: 25.6 us -> 22.6 us (0.88)
  Pallas kernels: 22.7 us -> 19.8 us
    pallas_call x1, Pallas kernels: 22.7 us -> 19.8 us  [fused(): pl.pallas_call(functools.partial(fused_kernel, n_blk, n_det, n_sub), out_...]
where the time goes in v3:
time: 22.6 us; the launch traced here: 22.5 us
  Pallas kernels  19.8 us (88%)
  local copies, waits for them, and re-layouts  2.04 us (9%)
  between operations  0.65 us (3%)
    pallas_call x1, Pallas kernels, fused(): pl.pallas_call(functools.partial(fused_kernel, n_blk, n_det, n_sub), out_...  19.8 us
    unnamed x4, local copies, waits for them, and re-layouts  2.04 us

profile of v3, /device:TPU:1, one launch (start us, length us, event | category | flops | bytes accessed | tf_op | source)
XLA Modules:
  0.0 22.5 jit_solution(9013936844592943177)
XLA Ops:
  0.6 19.8 %filter_and_chi.1 = (f32[8,1024]{1,0:T(8,128)}, f32[1,1,128,128]{3,2,1,0:T(8,128)}) custom-call(s32[1,1,128]{2,1,0:T(1,128)} %refs_0_.1, s32[1,1,128]{2,1,0:T(1,128)} %refs_1_.1, s32[1,1,128]{2,1,0:T(1,128)} %refs_2_.1, bf16[8,16,256]{2,1,0:T(8,128)(2,1)} %refs_3_.1, bf16[4,16,256]{2,1,0:T(8,128)(2,1)} %refs_4_.1, s32[4,15]{1,0:T(4,128)} %refs_5_.1, ...), custom_call_target="tpu_custom_call" | custom-call | tf_op jit(solution)/shard_map/filter_and_chi/pallas_call | solution.py:346
  20.4 0.0 copy-start
  20.4 1.4 %copy.16 = f32[8,1024]{1,0:T(8,128)} copy(f32[8,1024]{1,0:T(8,128)} %get-tuple-element.4) | data formatting | bytes 65536
  21.8 0.0 copy-done
  21.8 0.6 %copy.17 = f32[1,1,128,128]{3,2,1,0:T(8,128)} copy(f32[1,1,128,128]{3,2,1,0:T(8,128)S(1)} %copy-done) | data formatting | bytes 131072
Async XLA Ops:
  20.4 1.4 %copy-start = (f32[1,1,128,128]{3,2,1,0:T(8,128)S(1)}, f32[1,1,128,128]{3,2,1,0:T(8,128)}, u32[]{:S(2)}) copy-start(f32[1,1,128,128]{3,2,1,0:T(8,128)} %get-tuple-element.5) | copy-start | bytes 196612

commit v4 on v3

--- a/solution.py
+++ b/solution.py
@@ -76,7 +76,7 @@
     (ids_k_in, ids_p_in, ids_t_in, own_in, tmpl_in, cuts_in, first_in, twiddle_in, second_in, tile_dft_in,
      row_phase_in, tile_phase_in, peak_out, chi_out, data4, tmpl4, cuts, ids_k, ids_p, ids_t, first, twiddle,
      second, tile_dft, row_phase, tile_phase, cut_rows, cut_scr, cut_row_tab, cut_low_tab, norm_tab,
-     turn_tab, turned, hot_tab, before_tab, low_tab, spin_tab, scale_tab,
+     turn_tab, turned, hot_tab, before_tab, low_tab, spin_tab, scale_tab, best,
      local_sem, z_send, z_recv, x_send, x_recv, s_send, s_recv, tz_send, tz_recv, ts_send, ts_recv,
      cz_send, cz_recv) = refs
     f32, bf16 = jnp.float32, jnp.bfloat16
@@ -93,8 +93,18 @@
     own = b * n_det + d
 
     barrier = pltpu.get_barrier_semaphore()
-    for dz in range(1, n_blk):
-        pl.semaphore_signal(barrier, inc=1, device_id={"blk": lax.rem(b + dz, n_blk)}, device_id_type=MESH)
+    signs = (1, -1)
+
+    def has(sign):
+        return b < n_blk - 1 if sign == 1 else b > 0
+
+    def beside(sign):
+        return {"blk": lax.rem(b + sign + n_blk, n_blk)}
+
+    for sign in signs:
+        @pl.when(has(sign))
+        def _():
+            pl.semaphore_signal(barrier, inc=1, device_id=beside(sign), device_id_type=MESH)
     for dx in range(1, n_det):
         pl.semaphore_signal(barrier, inc=1, device_id={"det": lax.rem(d + dx, n_det)}, device_id_type=MESH)
     pl.semaphore_signal(barrier, inc=1, device_id={"sub": other}, device_id_type=MESH)
@@ -107,7 +117,7 @@
         copy.start()
     for copy in fetches[:3]:
         copy.wait()
-    pl.semaphore_wait(barrier, n_blk + n_det - 1)
+    pl.semaphore_wait(barrier, n_det + jnp.minimum(b, 1) + jnp.minimum(n_blk - 1 - b, 1))
 
     def remote(ref, send, recv, where):
         copy = pltpu.make_async_remote_copy(src_ref=ref, dst_ref=ref, send_sem=send, recv_sem=recv,
@@ -130,17 +140,56 @@
     def tmpl_half(place):
         return tmpl4.at[pl.ds(place * kb + half * hk, hk)]
 
-    z_copies, t_copies, c_copies, x_copies, s_copies, ts_copies = {}, {}, {}, {}, {}, {}
-    for dz in range(n_blk - 1, 0, -1):
-        where = {"blk": partner(dz)}
-        t_copies[dz] = remote(tmpl_half(b), tz_send.at[dz], tz_recv.at[dz], where)
-        c_copies[dz] = remote(cuts.at[b], cz_send.at[dz], cz_recv.at[dz], where)
-    for dz in range(n_blk - 1, 0, -1):
-        where = {"blk": partner(dz)}
-        z_copies[dz] = remote(data_half(own), z_send.at[dz], z_recv.at[dz], where)
+    def ref_of(kind, place):
+        if kind == 0:
+            return tmpl_half(place)
+        return cuts.at[place] if kind == 1 else data_half(place * n_det + d)
+
+    sends = (tz_send, cz_send, z_send)
+    recvs = (tz_recv, cz_recv, z_recv)
+
+    def hop(kind, sign, k):
+        side = signs.index(sign)
+        ref = ref_of(kind, b - sign * k)
+        return pltpu.make_async_remote_copy(
+            src_ref=ref, dst_ref=ref, send_sem=sends[kind].at[side, k], recv_sem=recvs[kind].at[side, k],
+            device_id=beside(sign), device_id_type=MESH)
+
+    def landed(kind, sign, k):
+        side = signs.index(sign)
+        ref = ref_of(kind, b - sign * k)
+        return pltpu.make_async_remote_copy(
+            src_ref=ref, dst_ref=ref, send_sem=sends[kind].at[side, k - 1], recv_sem=recvs[kind].at[side, k - 1],
+            device_id=beside(sign), device_id_type=MESH)
+
+    def holds(sign, k):
+        return b >= k if sign == 1 else b < n_blk - k
+
+    def x_hop(place, dx):
+        ref = data_half(place * n_det + d)
+        return pltpu.make_async_remote_copy(
+            src_ref=ref, dst_ref=ref, send_sem=x_send.at[place, dx], recv_sem=x_recv.at[place, dx],
+            device_id={"det": lax.rem(d + dx, n_det)}, device_id_type=MESH)
+
+    def s_hop(place, dx):
+        ref = data_half(place * n_det + lax.rem(d + n_det - dx, n_det))
+        return pltpu.make_async_remote_copy(
+            src_ref=ref, dst_ref=ref, send_sem=s_send.at[place, dx], recv_sem=s_recv.at[place, dx],
+            device_id={"sub": other}, device_id_type=MESH)
+
+    def ts_hop(place):
+        ref = tmpl_half(place)
+        return pltpu.make_async_remote_copy(
+            src_ref=ref, dst_ref=ref, send_sem=ts_send.at[place], recv_sem=ts_recv.at[place],
+            device_id={"sub": other}, device_id_type=MESH)
+
+    for kind in range(3):
+        for sign in signs:
+            @pl.when(has(sign))
+            def _():
+                hop(kind, sign, 0).start()
     for dx in range(1, n_det):
-        x_copies[0, dx] = remote(data_half(own), x_send.at[0, dx], x_recv.at[0, dx],
-                                 {"det": lax.rem(d + dx, n_det)})
+        x_hop(b, dx).start()
     for copy in fetches[3:]:
         copy.wait()
 
@@ -167,26 +216,40 @@
             power = snr[:n_half] * snr[:n_half] + snr[n_half:] * snr[n_half:]
             return jnp.maximum(peak, power * (1.0 / norm))
 
-        return lax.fori_loop(0, kb, one_template, peak, unroll=True)
-
-    peak = peak_of(b, jnp.zeros((n_half, pairs * NMAJ), f32))
-    for dz in range(n_blk - 1, 0, -1):
-        t_copies[dz].wait_recv()
-        src_b = partner(dz)
-        ts_copies[dz] = remote(tmpl_half(src_b), ts_send.at[dz], ts_recv.at[dz], {"sub": other})
-    for dz in range(n_blk - 1, 0, -1):
-        z_copies[dz].wait_recv()
-        src_b = partner(dz)
-        block = data_half(src_b * n_det + d)
-        for dx in range(1, n_det):
-            x_copies[dz, dx] = remote(block, x_send.at[dz, dx], x_recv.at[dz, dx],
-                                      {"det": lax.rem(d + dx, n_det)})
-        s_copies[dz, 0] = remote(block, s_send.at[dz, 0], s_recv.at[dz, 0], {"sub": other})
-        ts_copies[dz].wait_recv()
-        peak = peak_of(src_b, peak)
-
-    for copy in c_copies.values():
-        copy.wait_recv()
+        return lax.fori_loop(0, kb, one_template, peak, unroll=n_blk <= 4)
+
+    best[...] = peak_of(b, jnp.zeros((n_half, pairs * NMAJ), f32))
+
+    def peak_behind(k):
+        for sign in signs:
+            @pl.when(holds(sign, k))
+            def _():
+                place = b - sign * k
+                ts_hop(place).wait_recv()
+                best[...] = peak_of(place, best[...])
+
+    for k in range(1, n_blk):
+        for kind in range(3):
+            for sign in signs:
+                @pl.when(holds(sign, k))
+                def _():
+                    place = b - sign * k
+                    landed(kind, sign, k).wait_recv()
+
+                    @pl.when(has(sign))
+                    def _():
+                        hop(kind, sign, k).start()
+
+                    if kind == 0:
+                        ts_hop(place).start()
+                    if kind == 2:
+                        for dx in range(1, n_det):
+                            x_hop(place, dx).start()
+                        s_hop(place, 0).start()
+        if k > 1:
+            peak_behind(k - 1)
+    peak_behind(n_blk - 1)
+
     cut_rows[...] = jnp.full(cut_rows.shape, NMAJ * NMIN, jnp.int32)
     for blk in range(n_blk):
         cut_rows[blk * kb:(blk + 1) * kb, 0:n_cut] = cuts[blk]
@@ -228,21 +291,25 @@
         scale_tab[n] = norm_tab[k]
         return carry
 
-    order = [0] + list(range(n_blk - 1, 0, -1))
+    order = range(n_blk)
     bounds = [n_trig * i // n_blk for i in range(n_blk + 1)]
     for turn_at, dz in enumerate(order):
         lax.fori_loop(bounds[turn_at], bounds[turn_at + 1], prepare, 0, unroll=8)
         src_b = partner(dz)
         for dx in range(1, n_det):
-            x_copies[dz, dx].wait_recv()
-            block = data_half(src_b * n_det + lax.rem(d + n_det - dx, n_det))
-            s_copies[dz, dx] = remote(block, s_send.at[dz, dx], s_recv.at[dz, dx], {"sub": other})
-
-    swapped = swap_blocks(jnp.sqrt(peak))
-    for u in range(n_half // 8):
-        peak_out[:, u * 128:(u + 1) * 128] = swapped[8 * u:8 * u + 8, :]
-    for copy in s_copies.values():
-        copy.wait_recv()
+            x_hop(src_b, dx).wait_recv()
+            s_hop(src_b, dx).start()
+
+    swapped = swap_blocks(jnp.sqrt(best[...]))
+    peak_out[...] = swapped
+    for place in range(n_blk):
+        for dx in range(n_det):
+            if dx > 0:
+                s_hop(place, dx).wait_recv()
+            else:
+                @pl.when(b != place)
+                def _():
+                    s_hop(place, 0).wait_recv()
 
     sub = lax.broadcasted_iota(jnp.int32, (GROUP * NCUT, NMIN), 0) % NCUT
 
@@ -301,9 +368,21 @@
 
     lax.fori_loop(0, n_trig // GROUP, one_group, 0, unroll=8)
 
-    for group in (z_copies, t_copies, c_copies, x_copies, s_copies, ts_copies):
-        for copy in group.values():
-            copy.wait_send()
+    for k in range(n_blk):
+        for sign in signs:
+            @pl.when(jnp.logical_and(holds(sign, k), has(sign)))
+            def _():
+                for kind in range(3):
+                    hop(kind, sign, k).wait_send()
+    for place in range(n_blk):
+        for dx in range(1, n_det):
+            x_hop(place, dx).wait_send()
+            s_hop(place, dx).wait_send()
+
+        @pl.when(b != place)
+        def _():
+            s_hop(place, 0).wait_send()
+            ts_hop(place).wait_send()
 
 
 def fused(sizes, ids_k, ids_p, ids_t, own, tmpl, cuts, tables):
@@ -335,18 +414,19 @@
         pltpu.VMEM((n_trig, NCUT, NMIN), jnp.float32),
         pltpu.VMEM((n_trig, NCUT, 2 * NMIN), jnp.float32),
         pltpu.VMEM((n_trig, 1, NMIN), jnp.float32),
+        pltpu.VMEM((n_half, own.shape[0] * NMAJ), jnp.float32),
         dma((12,)),
-        dma((n_blk,)), dma((n_blk,)),
+        dma((2, n_blk)), dma((2, n_blk)),
         dma((n_blk, n_det)), dma((n_blk, n_det)),
         dma((n_blk, n_det)), dma((n_blk, n_det)),
+        dma((2, n_blk)), dma((2, n_blk)),
         dma((n_blk,)), dma((n_blk,)),
-        dma((n_blk,)), dma((n_blk,)),
-        dma((n_blk,)), dma((n_blk,)),
+        dma((2, n_blk)), dma((2, n_blk)),
     ]
     return pl.pallas_call(
         functools.partial(fused_kernel, n_blk, n_det, n_sub),
         out_shape=(
-            jax.ShapeDtypeStruct((own.shape[0], n_half * NMAJ), jnp.float32),
+            jax.ShapeDtypeStruct((n_half, own.shape[0] * NMAJ), jnp.float32),
             jax.ShapeDtypeStruct(ids_k.shape + (STEPS * NMAJ,), jnp.float32),
         ),
         in_specs=[anywhere] * 12,
@@ -362,6 +442,8 @@
 def body(sizes, data, templates, bin_cuts, trig_template, trig_pair, trig_tile):
     tables = tuple(jnp.asarray(t) for t in host_tables(sizes[2]))
     peak, chi = fused(sizes, trig_template, trig_pair, trig_tile, data, templates, bin_cuts, tables)
+    pairs = data.shape[0]
+    peak = peak.reshape(-1, pairs, peak.shape[1]).transpose(1, 0, 2).reshape(pairs, -1)
     return peak, chi
 
 

time: 22.6 us -> 24.7 us (1.093)
  Pallas kernels: 19.8 us -> 21.8 us
    pallas_call x1, Pallas kernels: 19.8 us -> 21.8 us  [fused(): pl.pallas_call(functools.partial(fused_kernel, n_blk, n_det, n_sub), out_...]
where the time goes in v4:
time: 24.7 us; the launch traced here: 24.5 us
  Pallas kernels  21.8 us (88%)
  local copies, waits for them, and re-layouts  2.04 us (8%)
  between operations  0.65 us (3%)
    pallas_call x1, Pallas kernels, fused(): pl.pallas_call(functools.partial(fused_kernel, n_blk, n_det, n_sub), out_...  21.8 us
    unnamed x4, local copies, waits for them, and re-layouts  2.04 us

profile of v4, /device:TPU:1, one launch (start us, length us, event | category | flops | bytes accessed | tf_op | source)
XLA Modules:
  0.0 24.5 jit_solution(3784704559866359146)
XLA Ops:
  0.6 21.8 %filter_and_chi.1 = (f32[64,128]{1,0:T(8,128)}, f32[1,1,128,128]{3,2,1,0:T(8,128)}) custom-call(s32[1,1,128]{2,1,0:T(1,128)} %refs_0_.1, s32[1,1,128]{2,1,0:T(1,128)} %refs_1_.1, s32[1,1,128]{2,1,0:T(1,128)} %refs_2_.1, bf16[8,16,256]{2,1,0:T(8,128)(2,1)} %refs_3_.1, bf16[4,16,256]{2,1,0:T(8,128)(2,1)} %refs_4_.1, s32[4,15]{1,0:T(4,128)} %refs_5_.1, ...), custom_call_target="tpu_custom_call" | custom-call | tf_op jit(solution)/shard_map/filter_and_chi/pallas_call | solution.py:426
  22.5 0.0 copy-start
  22.5 1.4 %copy.16 = f32[8,1024]{1,0:T(8,128)} copy(f32[8,1024]{1,0:T(8,128)} %bitcast.5) | data formatting | bytes 65536
  23.9 0.0 copy-done
  23.9 0.6 %copy.17 = f32[1,1,128,128]{3,2,1,0:T(8,128)} copy(f32[1,1,128,128]{3,2,1,0:T(8,128)S(1)} %copy-done) | data formatting | bytes 131072
Async XLA Ops:
  22.5 1.4 %copy-start = (f32[1,1,128,128]{3,2,1,0:T(8,128)S(1)}, f32[1,1,128,128]{3,2,1,0:T(8,128)}, u32[]{:S(2)}) copy-start(f32[1,1,128,128]{3,2,1,0:T(8,128)} %get-tuple-element.9) | copy-start | bytes 196612
